TPU v7x, 32 devices: a whole 2x2x4 slice. The times are simulated.
32 devices in a mesh: ens: 2 (over y), grid: 4 (over z), pole: 4 (over x, core).
Axes of the slice: x: 2, y: 2, z: 4, core: 2. Of those that a mesh axis runs over, the one named last changes fastest.
Arguments:
- inverse_pool: bfloat16 [8, 2, 4096, 4096], P(('ens', 'pole'), None, 'grid'), parts along dimension 0, may hold values from -6 to 6
- factor_tiles: bfloat16 [8, 4, 2, 10, 256, 256], P(('ens', 'pole'), None, None, None, 'grid'), parts along dimension 0, may hold values from -0.078125 to 0.078125
- diag_inverse: bfloat16 [8, 2, 1024, 256], P(('ens', 'pole'), None, 'grid'), parts along dimension 0, may hold values from -6 to 6
- pole_weight: float32 [4, 2], P('pole'), may hold values from -3 to 3
- ancestors: int32 [4, 10], replicated, may hold values from 0 to 15, all different within a row
Outputs:
- density_panel: float32 [8192, 1024], P(('ens', 'grid'), 'pole'), parts along dimension 0
- density_diagonal: float32 [2048, 256], P(('ens', 'grid')), parts along dimension 0
There are 2 independent parts, one for each index of `ens`. A program takes and returns all parts, laid end to end along the dimension named above; an argument that names none is the same for every part. Nothing has to cross between parts.
Inputs may be any that keep to these rules, and one draw needn't show every extreme that they name: `ancestors`: each row names 10 different ancestor blocks; every one of the 16 blocks is named by some row.
All inputs are finite; a program needn't handle non-finite values.
Results may differ from a plain program's by a relative error of at most 0.0022.
Values may be sent and summed in bfloat16 or wider, within the bound.
No kernel may reach another device: no remote copies, remote signals or barrier semaphores. Data moves between devices by JAX's collectives and lax.ppermute only.
A program may use at most 128 MiB of HBM per device.

v0:
```python
import functools

import jax
import jax.numpy as jnp
from jax import lax
from jax.experimental import pallas as pl
from jax.experimental.pallas import tpu as pltpu
from jax.sharding import PartitionSpec as P


def plain_product(left, right):
    return jnp.dot(left, right, preferred_element_type=jnp.float32)


def turned_product(left, right):
    return lax.dot_general(
        left, right, (((0,), (0,)), ((), ())), preferred_element_type=jnp.float32
    )


def portion_terms(rows_pair, block_index, offset, listed, factors, weights):
    tile_width = factors.shape[3]
    listed_count = factors.shape[1]
    height = rows_pair.shape[1]
    blocks = rows_pair.shape[2] // tile_width
    matches = listed == block_index

    def compute():
        chosen = rows_pair.reshape(2, height, blocks, tile_width)[:, :, listed, :].reshape(
            2, height, listed_count * tile_width
        )
        stacked = factors.reshape(2, listed_count * tile_width, tile_width)
        part_real = -(plain_product(chosen[0], stacked[0]) - plain_product(chosen[1], stacked[1]))
        part_imag = -(plain_product(chosen[0], stacked[1]) + plain_product(chosen[1], stacked[0]))
        panel_piece = weights[0] * part_imag + weights[1] * part_real
        rounded_real = part_real.astype(jnp.bfloat16)
        rounded_imag = part_imag.astype(jnp.bfloat16)
        position = jnp.sum(jnp.where(matches, jnp.arange(listed_count, dtype=jnp.int32), 0))
        matched = lax.dynamic_slice(
            factors, (jnp.int32(0), position, offset, jnp.int32(0)), (2, 1, height, tile_width)
        )[:, 0]
        diag_real = -(
            turned_product(matched[0], rounded_real) - turned_product(matched[1], rounded_imag)
        )
        diag_imag = -(
            turned_product(matched[0], rounded_imag) + turned_product(matched[1], rounded_real)
        )
        return (panel_piece, weights[0] * diag_imag + weights[1] * diag_real)

    def skipped():
        return (
            jnp.zeros((height, tile_width), jnp.float32),
            jnp.zeros((tile_width, tile_width), jnp.float32),
        )

    return lax.cond(jnp.any(matches), compute, skipped)


def rows_terms(rows_pair, row_first, listed, factors, weights):
    tile_width = factors.shape[3]
    height = rows_pair.shape[1]
    piece_rows = min(height, tile_width)
    panels = []
    diag_total = jnp.zeros((tile_width, tile_width), jnp.float32)
    for portion in range(height // piece_rows):
        row_start = row_first + portion * piece_rows
        panel_piece, diag_piece = portion_terms(
            rows_pair[:, portion * piece_rows : (portion + 1) * piece_rows],
            row_start // tile_width,
            row_start % tile_width,
            listed,
            factors,
            weights,
        )
        panels.append(panel_piece)
        diag_total = diag_total + diag_piece
    return (jnp.concatenate(panels, axis=0), diag_total)


def shards_any(inverse_pool, factor_tiles, diag_inverse, pole_weight, ancestors):
    device_index = lax.axis_index("grid")
    rows_here = inverse_pool.shape[2]
    supers = factor_tiles.shape[1]
    tile_width = factor_tiles.shape[5]
    row_slab = inverse_pool[0]
    weights = (pole_weight[0, 0], pole_weight[0, 1])
    row_first = device_index * rows_here
    own_panels = []
    diag_terms = []
    for supernode in range(supers):
        factors = lax.all_gather(factor_tiles[0, supernode], "grid", axis=2, tiled=True)
        listed = ancestors[supernode]
        own_panel, own_diag = rows_terms(row_slab, row_first, listed, factors, weights)
        diag_terms.append(own_diag)
        own_panels.append(own_panel)
    panel_rows = jnp.concatenate(own_panels, axis=1)
    panel_share = lax.psum_scatter(panel_rows, "pole", scatter_dimension=1, tiled=True)
    diag_term = jnp.stack(diag_terms, axis=0).reshape(supers * tile_width, tile_width)
    diag_local = diag_inverse[0]
    local_block = weights[0] * diag_local[1].astype(jnp.float32) + weights[1] * diag_local[
        0
    ].astype(jnp.float32)
    share_rows = local_block.shape[0]
    placed = lax.dynamic_update_slice(
        jnp.zeros_like(diag_term), local_block, (device_index * share_rows, jnp.int32(0))
    )
    spread = lax.psum_scatter(diag_term + placed, ("grid", "pole"), scatter_dimension=0, tiled=True)
    diag_share = lax.all_gather(spread, "pole", axis=0, tiled=True)
    return (panel_share, diag_share)


PAIRS_Z = [(0, 1), (1, 0), (2, 3), (3, 2)]
MIDDLE_Z = [(1, 2), (2, 1)]
OUTWARD_Z = [(1, 0), (2, 3)]
INWARD_Z = [(0, 1), (3, 2)]
ACROSS_X = [(0, 2), (2, 0), (1, 3), (3, 1)]
CHUNKS = ((0, 3), (1,), (2,))


ANYWHERE = pl.BlockSpec(memory_space=pl.ANY)
STAYING = pl.BlockSpec(memory_space=pltpu.MemorySpace.HBM)
SCALARS = pl.BlockSpec(memory_space=pltpu.SMEM)
WHOLE = pl.BlockSpec(memory_space=pltpu.VMEM)


def near_rows_kernel(table_ref, place_ref, tiles_ref, out_ref, sems):
    supers = out_ref.shape[0]
    slices = out_ref.shape[2]
    end_block = place_ref[3]

    def each(action):
        for k in range(supers):
            for part in range(slices):
                found = table_ref[k, end_block + part]

                @pl.when(found >= 0)
                def _(k=k, part=part, found=found):
                    action(
                        pltpu.make_async_copy(
                            tiles_ref.at[0, k, :, found],
                            out_ref.at[k, :, part],
                            sems.at[k, part],
                        )
                    )

    each(lambda copy: copy.start())
    each(lambda copy: copy.wait())


def pack_columns_kernel(depth, width, place_ref, pool_ref, out_ref):
    first_half = place_ref[2]
    blocks = pool_ref.shape[3] // width

    @pl.when(place_ref[1] == 1)
    def _():
        for offset, flag in ((depth, 1), (2 * depth, 0)):

            @pl.when(first_half == flag)
            def _(offset=offset):
                for part in range(2):
                    out_ref[part] = jnp.concatenate(
                        [
                            pool_ref[0, part, :, q * width + offset : q * width + offset + depth]
                            for q in range(blocks)
                        ],
                        axis=1,
                    )


def packed_columns(places, pool, depth, width, half, halves):
    height = pool.shape[2] // halves
    slices = pool.shape[2] // width
    tile = min(height, width)
    steps = height // tile
    groups = pool.shape[3] // (slices * width) - 1
    return pl.pallas_call(
        functools.partial(pack_columns_kernel, depth, width),
        out_shape=jax.ShapeDtypeStruct((2, height, groups * slices * depth), pool.dtype),
        grid_spec=pltpu.PrefetchScalarGridSpec(
            num_scalar_prefetch=1,
            grid=(steps, groups),
            in_specs=[
                pl.BlockSpec(
                    (1, 2, tile, slices * width),
                    lambda i, j, place: (0, 0, (half * steps + i) * place[1], (j + place[2]) * place[1]),
                )
            ],
            out_specs=pl.BlockSpec(
                (2, tile, slices * depth), lambda i, j, place: (0, i * place[1], j * place[1])
            ),
        ),
        cost_estimate=pl.CostEstimate(
            flops=0, bytes_accessed=3 * pool.shape[3] * height * 2, transcendentals=0
        ),
    )(places, pool)


def supernode_kernel(
    supernode,
    item_in_chunk,
    role,
    fresh,
    lent_item,
    table_ref,
    listed_ref,
    place_ref,
    weight_ref,
    pool_ref,
    tiles_ref,
    partner_ref,
    far_near_ref,
    far_far_ref,
    local_ref,
    *refs,
):
    columns_ref = None
    if lent_item is not None:
        columns_ref, *refs = refs
    diag_in_ref = refs[0] if fresh else refs[2]
    refs = refs[1:] if fresh else refs[3:]
    (
        sent_ref,
        kept_ref,
        diag_ref,
        factors,
        rows,
        out16,
        out32,
        total,
        columns,
        factor_sems,
        near_sems,
        row_sems,
        out_sems,
        diag_sem,
        column_sem,
    ) = refs
    width = total.shape[0]
    listed_count = factors.shape[0]
    slices = rows.shape[0]
    depth = tiles_ref.shape[4]
    place = place_ref[0]
    first_half = place_ref[2]
    end_block = place_ref[3]
    keeps = place_ref[5] == supernode // 2
    odd = lax.rem(place, 2)

    own_base = 2 * (1 - first_half)
    far_base = 2 * first_half
    near_slot = 1 - first_half
    near_start = pl.multiple_of((1 - odd + own_base) * depth, depth)
    pieces = [
        (tiles_ref.at[0, supernode], odd + own_base),
        (far_near_ref.at[item_in_chunk], near_slot + far_base),
        (far_far_ref.at[item_in_chunk], 1 - near_slot + far_base),
    ]
    if not role:
        pieces.append((partner_ref.at[item_in_chunk], 1 - odd + own_base))

    def each_piece(action):
        for number, (source, slot) in enumerate(pieces):
            start = pl.multiple_of(slot * depth, depth)
            for part in range(2):
                action(
                    pltpu.make_async_copy(
                        source.at[part],
                        factors.at[:, pl.ds(start, depth), pl.ds(part * width, width)],
                        factor_sems.at[number, part],
                    )
                )

    def each_near(action):
        @pl.loop(0, slices)
        def _(part):
            found = table_ref[supernode, place * slices + part]

            @pl.when(found >= 0)
            def _():
                for half in range(2):
                    action(
                        pltpu.make_async_copy(
                            partner_ref.at[supernode, half, part],
                            factors.at[found, pl.ds(near_start, depth), pl.ds(half * width, width)],
                            near_sems.at[part, half],
                        )
                    )

    def out_copy(part, action):
        panel_rows = pl.ds(pl.multiple_of(part * width, width), width)

        @pl.when(keeps)
        def _():
            action(
                pltpu.make_async_copy(out32.at[part], kept_ref.at[panel_rows, :], out_sems.at[part])
            )

        @pl.when(jnp.logical_not(keeps))
        def _():
            action(
                pltpu.make_async_copy(out16.at[part], sent_ref.at[panel_rows, :], out_sems.at[part])
            )

    @pl.when(place_ref[1] == role)
    def _():
        each_piece(lambda copy: copy.start())
        if role:
            each_near(lambda copy: copy.start())
        else:
            before = pltpu.make_async_copy(diag_in_ref.at[supernode], total, diag_sem)
            before.start()

        @pl.loop(0, slices)
        def _(part):
            @pl.when(table_ref[supernode, place * slices + part] >= 0)
            def _():
                @pl.loop(0, listed_count)
                def _(item):
                    column = pl.multiple_of(listed_ref[supernode, item] * width, width)
                    start = pl.multiple_of(part * width, width)
                    pltpu.make_async_copy(
                        pool_ref.at[0, :, pl.ds(start, width), pl.ds(column, width)],
                        rows.at[part, :, :, pl.ds(pl.multiple_of(item * width, width), width)],
                        row_sems.at[part],
                    ).start()

        if columns_ref is not None:
            lent_copy = pltpu.make_async_copy(columns_ref.at[lent_item], columns, column_sem)
            lent_copy.start()
        if role:

            @pl.loop(0, listed_count)
            def _(item):
                block = listed_ref[supernode, item]

                @pl.when(jnp.logical_or(block < end_block, block >= end_block + slices))
                def _():
                    factors[item, pl.ds(near_start, depth), :] = jnp.zeros(
                        (depth, 2 * width), factors.dtype
                    )

            total[...] = jnp.zeros(total.shape, total.dtype)
        else:
            before.wait()

        weight_real = weight_ref[0, 0]
        weight_imag = weight_ref[0, 1]

        @pl.when(place == supernode)
        def _():
            total[...] += weight_real * local_ref[0, 1].astype(jnp.float32) + weight_imag * local_ref[
                0, 0
            ].astype(jnp.float32)

        def add_diagonal(found, both):
            crossed = turned_product(factors[found], both)
            diag_real = -(crossed[:width, :width] - crossed[width:, width:])
            diag_imag = -(crossed[:width, width:] + crossed[width:, :width])
            total[...] += weight_real * diag_imag + weight_imag * diag_real

        each_piece(lambda copy: copy.wait())
        if role:
            each_near(lambda copy: copy.wait())

        @pl.loop(0, slices)
        def _(part):
            found = table_ref[supernode, place * slices + part]

            @pl.when(found < 0)
            def _():
                out32[part] = jnp.zeros((width, width), out32.dtype)
                out16[part] = jnp.zeros((width, width), out16.dtype)

            @pl.when(found >= 0)
            def _():
                pltpu.make_async_copy(
                    pool_ref.at[0, :, pl.ds(0, width), pl.ds(0, listed_count * width)],
                    rows.at[part],
                    row_sems.at[part],
                ).wait()
                stacked = factors[...].reshape(listed_count * 4 * depth, 2 * width)
                by_real = plain_product(rows[part, 0], stacked)
                by_imag = plain_product(rows[part, 1], stacked)
                real = -(by_real[:, :width] - by_imag[:, width:])
                imag = -(by_real[:, width:] + by_imag[:, :width])
                panel = weight_real * imag + weight_imag * real
                out32[part] = panel
                out16[part] = panel.astype(out16.dtype)
                add_diagonal(
                    found,
                    jnp.concatenate([real.astype(jnp.bfloat16), imag.astype(jnp.bfloat16)], axis=1),
                )

            out_copy(part, lambda copy: copy.start())

        if columns_ref is not None:
            lent_copy.wait()

            @pl.loop(0, columns.shape[0] // width)
            def _(part):
                found = table_ref[supernode, end_block + part]

                @pl.when(found >= 0)
                def _():
                    start = pl.multiple_of(part * width, width)
                    add_diagonal(found, columns[pl.ds(start, width), :])

        after = pltpu.make_async_copy(total, diag_ref.at[supernode], diag_sem)
        after.start()

        @pl.loop(0, slices)
        def _(part):
            out_copy(part, lambda copy: copy.wait())

        after.wait()


def supernode_terms(
    k, item, role, lent_item, table, listed, places, weights, pool, tiles, parts, local, columns, outputs
):
    width = tiles.shape[5]
    depth = tiles.shape[4]
    listed_count = tiles.shape[3]
    height = pool.shape[2]
    slices = height // width
    fresh = len(outputs) == 1
    first = 10 + len(columns)
    aliases = {first: 2} if fresh else {first + 2: 2, first: 0, first + 1: 1}
    lent_height = columns[0].shape[1] if columns else width
    return pl.pallas_call(
        functools.partial(supernode_kernel, k, item, role, fresh, lent_item),
        out_shape=(
            jax.ShapeDtypeStruct((height, width), jnp.bfloat16),
            jax.ShapeDtypeStruct((height, width), jnp.float32),
            jax.ShapeDtypeStruct((tiles.shape[1], width, width), jnp.float32),
        ),
        in_specs=[SCALARS] * 4
        + [STAYING] * 2
        + [ANYWHERE] * 3
        + [WHOLE]
        + [ANYWHERE] * (len(columns) + len(outputs)),
        out_specs=(ANYWHERE, ANYWHERE, ANYWHERE),
        input_output_aliases=aliases,
        scratch_shapes=[
            pltpu.VMEM((listed_count, 4 * depth, 2 * width), jnp.bfloat16),
            pltpu.VMEM((slices, 2, width, listed_count * width), jnp.bfloat16),
            pltpu.VMEM((slices, width, width), jnp.bfloat16),
            pltpu.VMEM((slices, width, width), jnp.float32),
            pltpu.VMEM((width, width), jnp.float32),
            pltpu.VMEM((lent_height, 2 * width), jnp.bfloat16),
            pltpu.SemaphoreType.DMA((4, 2)),
            pltpu.SemaphoreType.DMA((slices, 2)),
            pltpu.SemaphoreType.DMA((slices,)),
            pltpu.SemaphoreType.DMA((slices,)),
            pltpu.SemaphoreType.DMA,
            pltpu.SemaphoreType.DMA,
        ],
        compiler_params=pltpu.CompilerParams(vmem_limit_bytes=52 * 1024 * 1024),
        cost_estimate=pl.CostEstimate(
            flops=8 * height * width * width * listed_count,
            bytes_accessed=6 * height * width * listed_count,
            transcendentals=0,
        ),
    )(table, listed, places, weights, pool, tiles, *parts, local, *columns, *outputs)


def lent_kernel(
    half,
    known,
    table_ref,
    place_ref,
    weight_ref,
    columns_ref,
    tiles_ref,
    *refs,
):
    part_refs = [refs[3 * c : 3 * c + 3] for c in range(known)]
    refs = refs[3 * known :]
    diag_in_ref = None
    if half:
        diag_in_ref, *refs = refs
    (
        sent_ref,
        kept_ref,
        diag_ref,
        left_ref,
        columns,
        factors,
        matched,
        out16,
        out32,
        total,
        left,
        column_sem,
        factor_sems,
        matched_sems,
        out_sems,
        diag_sem,
        left_sem,
    ) = refs
    supers, width, _ = total.shape
    depth = tiles_ref.shape[4]
    slices = columns.shape[1] // width
    others = factors.shape[1] // depth
    place = place_ref[0]
    edge = place_ref[1]
    first_half = place_ref[2]
    end_block = place_ref[3]
    other_first = place_ref[4]
    chip = place_ref[5]
    weight_real = weight_ref[0, 0]
    weight_imag = weight_ref[0, 1]
    first_block = end_block + half * slices
    ready = [k for group in CHUNKS[:known] for k in group]
    pending = [k for k in range(supers) if k not in ready]

    @pl.when(edge == 0)
    def _():
        whole = pltpu.make_async_copy(columns_ref, columns, column_sem)
        whole.start()
        if half:
            before = pltpu.make_async_copy(diag_in_ref, total, diag_sem)
            before.start()

        @pl.loop(0, supers)
        def _(k):
            @pl.loop(0, others)
            def _(other):
                found = table_ref[k, other_first + other]
                span = pl.ds(pl.multiple_of(other * depth, depth), depth)

                @pl.when(found >= 0)
                def _():
                    for part in range(2):
                        pltpu.make_async_copy(
                            tiles_ref.at[0, k, part, found],
                            factors.at[k, span, pl.ds(part * width, width)],
                            factor_sems.at[k, other],
                        ).start()

                @pl.when(found < 0)
                def _():
                    factors[k, span, :] = jnp.zeros((depth, 2 * width), factors.dtype)

        for chunk, group in enumerate(CHUNKS[:known]):
            swap_ref, near_ref, far_ref = part_refs[chunk]
            for item, k in enumerate(group):

                @pl.loop(0, slices)
                def _(part, k=k, item=item, swap_ref=swap_ref, near_ref=near_ref, far_ref=far_ref):
                    found = table_ref[k, first_block + part]

                    @pl.when(found >= 0)
                    def _():
                        for source, slot in (
                            (tiles_ref.at[0, k], place),
                            (swap_ref.at[item], 3 * (1 - first_half)),
                            (near_ref.at[item], 1 + first_half),
                            (far_ref.at[item], 3 * first_half),
                        ):
                            start = pl.multiple_of(slot * depth, depth)
                            pltpu.make_async_copy(
                                source.at[:, found],
                                matched.at[k, part, :, pl.ds(start, depth), :],
                                matched_sems.at[k, part],
                            ).start()

        if half:
            before.wait()
        else:
            total[...] = jnp.zeros(total.shape, total.dtype)
        whole.wait()

        def out_copy(k, part, action):
            panel_rows = pl.ds(pl.multiple_of(part * width, width), width)
            slot = lax.rem(k, 2)

            @pl.when(chip == k // 2)
            def _():
                action(
                    pltpu.make_async_copy(
                        out32.at[slot, part], kept_ref.at[slot, panel_rows, :], out_sems.at[k, part]
                    )
                )

            @pl.when(chip != k // 2)
            def _():
                action(
                    pltpu.make_async_copy(
                        out16.at[slot, part], sent_ref.at[slot, panel_rows, :], out_sems.at[k, part]
                    )
                )

        @pl.loop(0, supers)
        def _(k):
            @pl.loop(0, others)
            def _(other):
                span = pl.ds(pl.multiple_of(other * depth, depth), depth)

                @pl.when(table_ref[k, other_first + other] >= 0)
                def _():
                    pltpu.make_async_copy(
                        factors.at[k, span, :], factors.at[k, span, :], factor_sems.at[k, other]
                    ).wait()

            slot = lax.rem(k, 2)
            mine = chip == k // 2

            @pl.loop(0, slices)
            def _(part):
                found = table_ref[k, first_block + part]
                panel_rows = pl.ds(pl.multiple_of(part * width, width), width)

                def store(panel):
                    @pl.when(mine)
                    def _():
                        out32[slot, part] = panel

                    @pl.when(jnp.logical_not(mine))
                    def _():
                        out16[slot, part] = panel.astype(out16.dtype)

                @pl.when(found < 0)
                def _():
                    store(jnp.zeros((width, width), jnp.float32))

                @pl.when(found >= 0)
                def _():
                    by_real = plain_product(columns[0, panel_rows, :], factors[k])
                    by_imag = plain_product(columns[1, panel_rows, :], factors[k])
                    real = -(by_real[:, :width] - by_imag[:, width:])
                    imag = -(by_real[:, width:] + by_imag[:, :width])
                    store(weight_real * imag + weight_imag * real)
                    both = jnp.concatenate(
                        [real.astype(jnp.bfloat16), imag.astype(jnp.bfloat16)], axis=1
                    )

                    def with_diagonal():
                        pltpu.make_async_copy(
                            matched.at[k, part], matched.at[k, part], matched_sems.at[k, part]
                        ).wait()
                        crossed_real = turned_product(matched[k, part, 0], both)
                        crossed_imag = turned_product(matched[k, part, 1], both)
                        diag_real = -(crossed_real[:, :width] - crossed_imag[:, width:])
                        diag_imag = -(crossed_real[:, width:] + crossed_imag[:, :width])
                        total[k] += weight_real * diag_imag + weight_imag * diag_real

                    if pending:
                        is_pending = functools.reduce(jnp.logical_or, [k == p for p in pending])
                        pl.when(jnp.logical_not(is_pending))(with_diagonal)
                        place_in = sum(
                            jnp.where(k == p, index, 0) for index, p in enumerate(pending)
                        )

                        @pl.when(is_pending)
                        def _():
                            left[place_in, panel_rows, :] = both
                    else:
                        with_diagonal()

                out_copy(k, part, lambda copy: copy.start())

        after = pltpu.make_async_copy(total, diag_ref, diag_sem)
        after.start()
        if pending:
            keep = pltpu.make_async_copy(left, left_ref, left_sem)
            keep.start()
            keep.wait()

        @pl.loop(0, supers)
        def _(k):
            @pl.loop(0, slices)
            def _(part):
                out_copy(k, part, lambda copy: copy.wait())

        after.wait()


def lent_terms(half, known, table, places, weights, columns, tiles, parts, outputs):
    supers = tiles.shape[1]
    width = tiles.shape[5]
    depth = tiles.shape[4]
    height = columns.shape[1]
    slices = height // width
    others = columns.shape[2] // depth
    left = max(1, supers - sum(len(group) for group in CHUNKS[:known]))
    left_shape = (left, height, 2 * width)
    return pl.pallas_call(
        functools.partial(lent_kernel, half, known),
        out_shape=(
            jax.ShapeDtypeStruct((2, height, width), jnp.bfloat16),
            jax.ShapeDtypeStruct((2, height, width), jnp.float32),
            jax.ShapeDtypeStruct((supers, width, width), jnp.float32),
            jax.ShapeDtypeStruct(left_shape, jnp.bfloat16),
        ),
        in_specs=[SCALARS] * 3 + [ANYWHERE] * (2 + 3 * known + len(outputs)),
        out_specs=(ANYWHERE,) * 4,
        input_output_aliases={5 + 3 * known: 2} if outputs else {},
        scratch_shapes=[
            pltpu.VMEM(columns.shape, columns.dtype),
            pltpu.VMEM((supers, others * depth, 2 * width), tiles.dtype),
            pltpu.VMEM((supers, slices, 2, 4 * depth, width), tiles.dtype),
            pltpu.VMEM((2, slices, width, width), jnp.bfloat16),
            pltpu.VMEM((2, slices, width, width), jnp.float32),
            pltpu.VMEM((supers, width, width), jnp.float32),
            pltpu.VMEM(left_shape, jnp.bfloat16),
            pltpu.SemaphoreType.DMA,
            pltpu.SemaphoreType.DMA((supers, others)),
            pltpu.SemaphoreType.DMA((supers, slices)),
            pltpu.SemaphoreType.DMA((supers, slices)),
            pltpu.SemaphoreType.DMA,
            pltpu.SemaphoreType.DMA,
        ],
        compiler_params=pltpu.CompilerParams(vmem_limit_bytes=52 * 1024 * 1024),
        cost_estimate=pl.CostEstimate(
            flops=8 * height * supers * width * others * depth,
            bytes_accessed=8 * supers * others * depth * width,
            transcendentals=0,
        ),
    )(table, places, weights, columns, tiles, *parts, *outputs)


def shards_line(inverse_pool, factor_tiles, diag_inverse, pole_weight, ancestors):
    supers = factor_tiles.shape[1]
    listed_count = factor_tiles.shape[3]
    depth = factor_tiles.shape[4]
    width = factor_tiles.shape[5]
    height = inverse_pool.shape[2]
    slices = height // width
    blocks = inverse_pool.shape[3] // width
    place = lax.axis_index("grid")
    pole = lax.axis_index("pole")
    chip = pole // 2
    core = pole % 2
    edge = jnp.logical_or(place == 0, place == 3)
    first_half = (place < 2).astype(jnp.int32)
    places = jnp.stack(
        [place, edge.astype(jnp.int32), first_half, 3 * slices * (1 - first_half), slices * first_half, chip]
    ).astype(jnp.int32)
    same = ancestors[:, :, None] == jnp.arange(blocks, dtype=jnp.int32)
    table = jnp.max(
        jnp.where(same, jnp.arange(listed_count, dtype=jnp.int32)[None, :, None], -1), axis=1
    ).astype(jnp.int32)

    def planes(places_z, pairs):
        return [(4 * z + a, 4 * z + b) for z in places_z for a, b in pairs]

    def halves(value, which, axis):
        size = value.shape[axis] // 2
        return (
            lax.dynamic_slice_in_dim(value, (1 - which) * size, size, axis),
            lax.dynamic_slice_in_dim(value, which * size, size, axis),
        )

    def joined(mine, other, which):
        return jnp.where(which == 0, jnp.concatenate([mine, other]), jnp.concatenate([other, mine]))

    owns = [jnp.stack([factor_tiles[0, k] for k in group]) for group in CHUNKS]
    near_rows = pl.pallas_call(
        near_rows_kernel,
        out_shape=jax.ShapeDtypeStruct((supers, 2, slices, depth, width), factor_tiles.dtype),
        in_specs=[SCALARS] * 2 + [ANYWHERE],
        out_specs=WHOLE,
        scratch_shapes=[pltpu.SemaphoreType.DMA((supers, slices))],
        name="near_rows",
    )(table, places, factor_tiles)
    near = lax.ppermute(near_rows, "grid", OUTWARD_Z)
    lent = []
    for half in range(2):
        packed = packed_columns(places, inverse_pool, depth, width, half, 2)
        lent.append(lax.ppermute(packed, "grid", INWARD_Z))

    parts = []
    for own in owns:
        swap = lax.ppermute(own, "grid", INWARD_Z)
        mid_near = lax.ppermute(own, "grid", MIDDLE_Z)
        mid_far = lax.ppermute(swap, "grid", MIDDLE_Z)
        end_near = lax.ppermute(mid_near, "grid", OUTWARD_Z)
        end_far = lax.ppermute(mid_far, "grid", OUTWARD_Z)
        parts.append((swap, mid_near, mid_far, end_near, end_far))

    both_axes = ("grid", "pole")
    middles = [piece for part in parts for piece in part[:3]]
    common = (table, ancestors, places, pole_weight, inverse_pool, factor_tiles)

    def node(k, role, columns, outputs):
        c = next(c for c, group in enumerate(CHUNKS) if k in group)
        swap, mid_near, mid_far, end_near, end_far = parts[c]
        wanted = (near, end_near, end_far) if role else (swap, mid_near, mid_far)
        return supernode_terms(
            k, CHUNKS[c].index(k), role, k - 1 if columns else None, *common, wanted,
            diag_inverse, columns, outputs,
        )

    def lent_node(half, known, outputs):
        return lent_terms(
            half, known, table, places, pole_weight, lent[half], factor_tiles,
            middles[: 3 * known], outputs,
        )

    lent_sent, lent_kept = [None] * 2, [None] * 2
    lent_sent[0], lent_kept[0], diag, columns = lent_node(0, 1, ())
    outer = node(0, 0, (), (diag,))
    outer = node(3, 0, (), outer)
    outer = node(0, 1, (), outer)
    sent_outer, kept_outer, diag = node(3, 1, (), outer)
    inner = node(1, 0, (columns,), (diag,))
    inner = node(2, 0, (columns,), inner)
    lent_sent[1], lent_kept[1], diag, _ = lent_node(1, len(CHUNKS), (inner[2],))
    sent_inner, kept_inner, diag = node(1, 1, (), (inner[0], inner[1], diag))
    sent_inner, kept_inner, diag = node(2, 1, (), (sent_inner, kept_inner, diag))

    returned = []
    for half in range(2):
        both = lent_kept[half] + lax.ppermute(
            lent_sent[half], both_axes, planes((1, 2), ACROSS_X)
        ).astype(jnp.float32)
        mine = jnp.where(core == 0, both[0], both[1])
        yours = jnp.where(core == 0, both[1], both[0])
        mine = mine + lax.ppermute(yours, both_axes, planes((1, 2), PAIRS_Z))
        returned.append(lax.ppermute(mine.astype(jnp.bfloat16), "grid", OUTWARD_Z))

    chip_sum = kept_outer + lax.ppermute(sent_outer, "pole", ACROSS_X).astype(jnp.float32)
    base = chip_sum + lax.ppermute(chip_sum, "pole", [(1, 0), (2, 3)])
    in_outer = jnp.logical_or(pole == 0, pole == 3)
    back = jnp.concatenate(returned).astype(jnp.float32)
    base = jnp.where(in_outer, base, 0.0) + jnp.where(edge, back, 0.0)
    base = lax.optimization_barrier(base)
    chip_sum = kept_inner + lax.ppermute(sent_inner, "pole", ACROSS_X).astype(jnp.float32)
    last = chip_sum + lax.ppermute(chip_sum, "pole", [(0, 1), (3, 2)])
    panel_share = base + jnp.where(in_outer, 0.0, last)

    def to_quarters(value, places_z):
        sent, kept = halves(value, core, 1)
        value = kept + lax.ppermute(sent, both_axes, planes(places_z, PAIRS_Z))
        sent, kept = halves(value, chip, 1)
        return kept + lax.ppermute(sent, both_axes, planes(places_z, ACROSS_X))

    quarters = to_quarters(diag, range(4))
    own = lax.dynamic_index_in_dim(quarters, place, 0, keepdims=False)
    for shift in range(1, 4):
        sent = lax.dynamic_index_in_dim(quarters, (place + shift) % 4, 0, keepdims=False)
        own = own + lax.ppermute(sent, "grid", [(z, (z + shift) % 4) for z in range(4)])
    own = joined(own, lax.ppermute(own, "pole", ACROSS_X), chip)
    diag_share = joined(own, lax.ppermute(own, "pole", PAIRS_Z), core)
    return (panel_share, diag_share)


def solution(mesh):
    in_specs = (
        P(("ens", "pole"), None, "grid", None),
        P(("ens", "pole"), None, None, None, "grid", None),
        P(("ens", "pole"), None, "grid", None),
        P("pole", None),
        P(),
    )
    out_specs = (P(("ens", "grid"), "pole"), P(("ens", "grid"), None))

    def shards(inverse_pool, factor_tiles, diag_inverse, pole_weight, ancestors):
        groups = mesh.shape["grid"]
        poles = mesh.shape["pole"]
        supers = factor_tiles.shape[1]
        width = factor_tiles.shape[5]
        line = (
            groups == 4
            and poles == 4
            and supers == 4
            and factor_tiles.shape[4] * groups == width
            and inverse_pool.shape[2] % width == 0
            and diag_inverse.shape[2] == width
            and width % 256 == 0
        )
        if not line:
            return shards_any(inverse_pool, factor_tiles, diag_inverse, pole_weight, ancestors)
        return shards_line(inverse_pool, factor_tiles, diag_inverse, pole_weight, ancestors)

    return jax.shard_map(shards, mesh=mesh, in_specs=in_specs, out_specs=out_specs, check_vma=False)
```

profile of v0, /device:TPU:0, one launch (start us, length us, event | category | flops | bytes accessed | tf_op | source)
XLA Modules:
  0.0 305.7 jit_solution(1197509234661411469)
XLA Ops:
  0.6 3.0 slice_bitcast_fusion
  4.9 5.0 %collective-permute-start.3 = (bf16[2,2,10,64,256]{4,3,2,1,0:T(8,128)(2,1)}, bf16[2,2,10,64,256]{4,3,2,1,0:T(8,128)(2,1)S(1)}, u32[]{:S(2)}, u32[]{:S(2)}) collective-permute-start(bf16[2,2,10,64,256]{4,3,2,1,0:T(8,128)(2,1)} %pad_maximum_fusion), channel_id=1, source_target_pairs={{0,4},{12,8},{1,5},{13,9},{2,6},{14,10},{3,7},{15,11},{16,20},{28,... | collective-permute-start | bytes 3932168 | tf_op jit(solution)/shard_map/ppermute | solution.py:774
  12.3 6.7 %shard_map.68 = bf16[2,512,768]{2,1,0:T(8,128)(2,1)} custom-call(s32[6]{0:T(128)} %stack.34.place_ref, bf16[1,2,1024,4096]{3,2,1,0:T(8,128)(2,1)} %pool_ref.19), custom_call_target="tpu_custom_call" | custom-call | bytes 12582912 | tf_op jit(solution)/shard_map/pallas_call | solution.py:176
  19.0 2.5 collective-permute-start.6
  21.5 17.8 %collective-permute-done.3.refs_0_.partner_ref = bf16[2,2,10,64,256]{4,3,2,1,0:T(8,128)(2,1)S(1)} collective-permute-done((bf16[2,2,10,64,256]{4,3,2,1,0:T(8,128)(2,1)}, bf16[2,2,10,64,256]{4,3,2,1,0:T(8,128)(2,1)S(1)}, u32[]{:S(2)}, u32[]{:S(2)}) %collective-permute-start.3) | collective-permute-done | bytes 1310752 | tf_op jit(solution)/shard_map/ppermute | solution.py:774
  41.0 6.0 %collective-permute-start.13 = (bf16[1,2,10,64,256]{4,3,2,1,0:T(8,128)(2,1)}, bf16[1,2,10,64,256]{4,3,2,1,0:T(8,128)(2,1)S(1)}, u32[]{:S(2)}, u32[]{:S(2)}) collective-permute-start(bf16[1,2,10,64,256]{4,3,2,1,0:T(8,128)(2,1)} %get-tuple-element.65), channel_id=1, source_target_pairs={{0,4},{12,8},{1,5},{13,9},{2,6},{14,10},{3,7},{15,11},{16,20},{28,... | collective-permute-start | bytes 1966088 | tf_op jit(solution)/shard_map/ppermute | solution.py:774
  51.0 22.0 %collective-permute-done.6.columns_ref = bf16[2,512,768]{2,1,0:T(8,128)(2,1)} collective-permute-done((bf16[2,512,768]{2,1,0:T(8,128)(2,1)}, bf16[2,512,768]{2,1,0:T(8,128)(2,1)}, u32[]{:S(2)}, u32[]{:S(2)}) %collective-permute-start.6) | collective-permute-done | bytes 1572896 | tf_op jit(solution)/shard_map/ppermute | solution.py:770
  77.2 3.0 near_rows.1
  80.2 6.8 %shard_map.74 = bf16[2,512,768]{2,1,0:T(8,128)(2,1)} custom-call(s32[6]{0:T(128)} %stack.34.place_ref, bf16[1,2,1024,4096]{3,2,1,0:T(8,128)(2,1)} %pool_ref.19), custom_call_target="tpu_custom_call" | custom-call | bytes 12582912 | tf_op jit(solution)/shard_map/pallas_call | solution.py:176
  89.6 10.3 %collective-permute-done.16.partner_ref.refs_6_ = bf16[1,2,10,64,256]{4,3,2,1,0:T(8,128)(2,1)S(1)} collective-permute-done((bf16[1,2,10,64,256]{4,3,2,1,0:T(8,128)(2,1)}, bf16[1,2,10,64,256]{4,3,2,1,0:T(8,128)(2,1)S(1)}, u32[]{:S(2)}, u32[]{:S(2)}) %collective-permute-start.16) | collective-permute-done | bytes 655392 | tf_op jit(solution)/shard_map/ppermute | solution.py:774
  106.9 16.6 %collective-permute-done.partner_ref = bf16[4,2,4,64,256]{4,3,2,1,0:T(8,128)(2,1)S(1)} collective-permute-done((bf16[4,2,4,64,256]{4,3,2,1,0:T(8,128)(2,1)}, bf16[4,2,4,64,256]{4,3,2,1,0:T(8,128)(2,1)S(1)}, u32[]{:S(2)}, u32[]{:S(2)}) %collective-permute-start) | collective-permute-done | bytes 1048608 | tf_op jit(solution)/shard_map/ppermute | solution.py:766
  123.6 8.1 %collective-permute-start.12 = (bf16[2,512,768]{2,1,0:T(8,128)(2,1)}, bf16[2,512,768]{2,1,0:T(8,128)(2,1)S(1)}, u32[]{:S(2)}, u32[]{:S(2)}) collective-permute-start(bf16[2,512,768]{2,1,0:T(8,128)(2,1)} %shard_map.74), channel_id=1, source_target_pairs={{0,4},{12,8},{1,5},{13,9},{2,6},{14,10},{3,7},{15,11},{16,20},{28,... | collective-permute-start | bytes 4718600 | tf_op jit(solution)/shard_map/ppermute | solution.py:770
  134.3 17.3 %collective-permute-done.2.far_near_ref = bf16[2,2,10,64,256]{4,3,2,1,0:T(8,128)(2,1)S(1)} collective-permute-done((bf16[2,2,10,64,256]{4,3,2,1,0:T(8,128)(2,1)}, bf16[2,2,10,64,256]{4,3,2,1,0:T(8,128)(2,1)S(1)}, u32[]{:S(2)}, u32[]{:S(2)}) %collective-permute-start.2) | collective-permute-done | bytes 1310752 | tf_op jit(solution)/shard_map/ppermute | solution.py:777
  152.9 26.8 %collective-permute-done.5.far_far_ref = bf16[2,2,10,64,256]{4,3,2,1,0:T(8,128)(2,1)S(1)} collective-permute-done((bf16[2,2,10,64,256]{4,3,2,1,0:T(8,128)(2,1)}, bf16[2,2,10,64,256]{4,3,2,1,0:T(8,128)(2,1)S(1)}, u32[]{:S(2)}, u32[]{:S(2)}) %collective-permute-start.5) | collective-permute-done | bytes 1310752 | tf_op jit(solution)/shard_map/ppermute | solution.py:778
  181.1 9.5 %shard_map.72 = (bf16[1024,256]{1,0:T(8,128)(2,1)S(1)}, f32[1024,256]{1,0:T(8,128)S(1)}, f32[4,256,256]{2,1,0:T(8,128)}) custom-call(s32[4,16]{1,0:T(4,128)S(1)} %copy-done.6, s32[4,10]{1,0:T(4,128)S(1)} %copy-done.7, s32[6]{0:T(128)S(1)} %copy-done.9, f32[1,2]{1,0:T(1,128)S(1)} %copy-done.10, ...), custom_call_target="tpu_custom_call", output_to_operand_aliasing={{2}: (12, {}), {0}: (10, {}), {1}: (11, {})} | custom-call | flops 5368709120 | bytes 15728640 | tf_op jit(solution)/shard_map/pallas_call | solution.py:429
  190.5 8.1 %shard_map.73 = (bf16[1024,256]{1,0:T(8,128)(2,1)S(1)}, f32[1024,256]{1,0:T(8,128)S(1)}, f32[4,256,256]{2,1,0:T(8,128)}) custom-call(s32[4,16]{1,0:T(4,128)S(1)} %copy-done.6, s32[4,10]{1,0:T(4,128)S(1)} %copy-done.7, s32[6]{0:T(128)S(1)} %copy-done.9, f32[1,2]{1,0:T(1,128)S(1)} %copy-done.10, ...), custom_call_target="tpu_custom_call", output_to_operand_aliasing={{2}: (12, {}), {0}: (10, {}), {1}: (11, {})} | custom-call | flops 5368709120 | bytes 15728640 | tf_op jit(solution)/shard_map/pallas_call | solution.py:429
  203.3 18.7 %collective-permute-done.25.far_far_ref = bf16[1,2,10,64,256]{4,3,2,1,0:T(8,128)(2,1)} collective-permute-done((bf16[1,2,10,64,256]{4,3,2,1,0:T(8,128)(2,1)S(1)}, bf16[1,2,10,64,256]{4,3,2,1,0:T(8,128)(2,1)}, u32[]{:S(2)}, u32[]{:S(2)}) %collective-permute-start.25) | collective-permute-done | bytes 655392 | tf_op jit(solution)/shard_map/ppermute | solution.py:778
  222.0 9.4 %shard_map.78 = (bf16[1024,256]{1,0:T(8,128)(2,1)S(1)}, f32[1024,256]{1,0:T(8,128)}, f32[4,256,256]{2,1,0:T(8,128)}) custom-call(s32[4,16]{1,0:T(4,128)S(1)} %copy-done.6, s32[4,10]{1,0:T(4,128)S(1)} %copy-done.7, s32[6]{0:T(128)S(1)} %copy-done.9, f32[1,2]{1,0:T(1,128)S(1)} %copy-done.10, ...), custom_call_target="tpu_custom_call", output_to_operand_aliasing={{2}: (12, {}), {0}: (10, {}), {1}: (11, {})} | custom-call | flops 5368709120 | bytes 15728640 | tf_op jit(solution)/shard_map/pallas_call | solution.py:429
  232.6 11.7 %shard_map.79 = (bf16[1024,256]{1,0:T(8,128)(2,1)S(1)}, f32[1024,256]{1,0:T(8,128)}, f32[4,256,256]{2,1,0:T(8,128)}) custom-call(s32[4,16]{1,0:T(4,128)S(1)} %copy-done.6, s32[4,10]{1,0:T(4,128)S(1)} %copy-done.7, s32[6]{0:T(128)S(1)} %copy-done.9, f32[1,2]{1,0:T(1,128)S(1)} %copy-done.10, ...), custom_call_target="tpu_custom_call", output_to_operand_aliasing={{2}: (12, {}), {0}: (10, {}), {1}: (11, {})} | custom-call | flops 5368709120 | bytes 15728640 | tf_op jit(solution)/shard_map/pallas_call | solution.py:429
  253.4 21.9 %collective-permute-done.7 = bf16[1024,256]{1,0:T(8,128)(2,1)S(1)} collective-permute-done((bf16[1024,256]{1,0:T(8,128)(2,1)S(1)}, bf16[1024,256]{1,0:T(8,128)(2,1)S(1)}, u32[]{:S(2)}, u32[]{:S(2)}) %collective-permute-start.7) | collective-permute-done | bytes 524320 | tf_op jit(solution)/shard_map/ppermute | solution.py:822
  276.8 3.6 %collective-permute-done.29 = f32[4,64,256]{2,1,0:T(8,128)S(1)} collective-permute-done((f32[4,64,256]{2,1,0:T(8,128)S(1)}, f32[4,64,256]{2,1,0:T(8,128)S(1)}, u32[]{:S(2)}, u32[]{:S(2)}) %collective-permute-start.29) | collective-permute-done | bytes 262176 | tf_op jit(solution)/shard_map/ppermute | solution.py:836
  280.7 3.7 %collective-permute-start.32 = (f32[64,256]{1,0:T(8,128)S(1)}, f32[64,256]{1,0:T(8,128)S(1)}, u32[]{:S(2)}, u32[]{:S(2)}) collective-permute-start(f32[64,256]{1,0:T(8,128)S(1)} %get-tuple-element.69), channel_id=1, source_target_pairs={{0,12},{4,0},{8,4},{12,8},{1,13},{5,1},{9,5},{13,9},{2,14},{6,2},{... | collective-permute-start | bytes 196616 | tf_op jit(solution)/shard_map/ppermute | solution.py:842
  284.5 2.8 collective-permute-done.30
  296.6 6.3 %collective-permute-done.21 = bf16[512,256]{1,0:T(8,128)(2,1)} collective-permute-done((bf16[512,256]{1,0:T(8,128)(2,1)}, bf16[512,256]{1,0:T(8,128)(2,1)}, u32[]{:S(2)}, u32[]{:S(2)}) %collective-permute-start.21) | collective-permute-done | bytes 262176 | tf_op jit(solution)/shard_map/ppermute | solution.py:820
  (126 shorter events, 56.7 us)
Async XLA Ops:
  4.9 34.4 %collective-permute-start.3 = (bf16[2,2,10,64,256]{4,3,2,1,0:T(8,128)(2,1)}, bf16[2,2,10,64,256]{4,3,2,1,0:T(8,128)(2,1)S(1)}, u32[]{:S(2)}, u32[]{:S(2)}) collective-permute-start(bf16[2,2,10,64,256]{4,3,2,1,0:T(8,128)(2,1)} %pad_maximum_fusion), channel_id=1, source_target_pairs={{0,4},{12,8},{1,5},{13,9},{2,6},{14,10},{3,7},{15,11},{16,20},{28,... | collective-permute-start | bytes 3932168 | tf_op jit(solution)/shard_map/ppermute | solution.py:774
  9.9 38.7 %collective-permute-start.1 = (bf16[2,2,10,64,256]{4,3,2,1,0:T(8,128)(2,1)}, bf16[2,2,10,64,256]{4,3,2,1,0:T(8,128)(2,1)}, u32[]{:S(2)}, u32[]{:S(2)}) collective-permute-start(bf16[2,2,10,64,256]{4,3,2,1,0:T(8,128)(2,1)} %pad_maximum_fusion), channel_id=1, source_target_pairs={{4,8},{8,4},{5,9},{9,5},{6,10},{10,6},{7,11},{11,7},{20,24},{24,20... | collective-permute-start | bytes 3932168 | tf_op jit(solution)/shard_map/ppermute | solution.py:775
  19.0 54.0 %collective-permute-start.6 = (bf16[2,512,768]{2,1,0:T(8,128)(2,1)}, bf16[2,512,768]{2,1,0:T(8,128)(2,1)}, u32[]{:S(2)}, u32[]{:S(2)}) collective-permute-start(bf16[2,512,768]{2,1,0:T(8,128)(2,1)} %shard_map.68), channel_id=1, source_target_pairs={{0,4},{12,8},{1,5},{13,9},{2,6},{14,10},{3,7},{15,11},{16,20},{28,... | collective-permute-start | bytes 4718600 | tf_op jit(solution)/shard_map/ppermute | solution.py:770
  39.3 35.2 %collective-permute-start.4 = (bf16[2,2,10,64,256]{4,3,2,1,0:T(8,128)(2,1)S(1)}, bf16[2,2,10,64,256]{4,3,2,1,0:T(8,128)(2,1)}, u32[]{:S(2)}, u32[]{:S(2)}) collective-permute-start(bf16[2,2,10,64,256]{4,3,2,1,0:T(8,128)(2,1)S(1)} %collective-permute-done.3.refs_0_.partner_ref), channel_id=1, source_target_pairs={{4,8},{8,4},{5,9},{9,5},{6,10},{10,6},{7,11},{11,7},{20,24},{24,20... | collective-permute-start | bytes 3932168 | tf_op jit(solution)/shard_map/ppermute | solution.py:776
  41.0 46.0 %collective-permute-start.13 = (bf16[1,2,10,64,256]{4,3,2,1,0:T(8,128)(2,1)}, bf16[1,2,10,64,256]{4,3,2,1,0:T(8,128)(2,1)S(1)}, u32[]{:S(2)}, u32[]{:S(2)}) collective-permute-start(bf16[1,2,10,64,256]{4,3,2,1,0:T(8,128)(2,1)} %get-tuple-element.65), channel_id=1, source_target_pairs={{0,4},{12,8},{1,5},{13,9},{2,6},{14,10},{3,7},{15,11},{16,20},{28,... | collective-permute-start | bytes 1966088 | tf_op jit(solution)/shard_map/ppermute | solution.py:774
  47.1 41.2 %collective-permute-start.14 = (bf16[1,2,10,64,256]{4,3,2,1,0:T(8,128)(2,1)}, bf16[1,2,10,64,256]{4,3,2,1,0:T(8,128)(2,1)}, u32[]{:S(2)}, u32[]{:S(2)}) collective-permute-start(bf16[1,2,10,64,256]{4,3,2,1,0:T(8,128)(2,1)} %get-tuple-element.65), channel_id=1, source_target_pairs={{4,8},{8,4},{5,9},{9,5},{6,10},{10,6},{7,11},{11,7},{20,24},{24,20... | collective-permute-start | bytes 1966088 | tf_op jit(solution)/shard_map/ppermute | solution.py:775
  48.6 51.3 %collective-permute-start.16 = (bf16[1,2,10,64,256]{4,3,2,1,0:T(8,128)(2,1)}, bf16[1,2,10,64,256]{4,3,2,1,0:T(8,128)(2,1)S(1)}, u32[]{:S(2)}, u32[]{:S(2)}) collective-permute-start(bf16[1,2,10,64,256]{4,3,2,1,0:T(8,128)(2,1)} %get-tuple-element.64), channel_id=1, source_target_pairs={{0,4},{12,8},{1,5},{13,9},{2,6},{14,10},{3,7},{15,11},{16,20},{28,... | collective-permute-start | bytes 1966088 | tf_op jit(solution)/shard_map/ppermute | solution.py:774
  73.0 29.2 %collective-permute-start.17 = (bf16[1,2,10,64,256]{4,3,2,1,0:T(8,128)(2,1)}, bf16[1,2,10,64,256]{4,3,2,1,0:T(8,128)(2,1)}, u32[]{:S(2)}, u32[]{:S(2)}) collective-permute-start(bf16[1,2,10,64,256]{4,3,2,1,0:T(8,128)(2,1)} %get-tuple-element.64), channel_id=1, source_target_pairs={{4,8},{8,4},{5,9},{9,5},{6,10},{10,6},{7,11},{11,7},{20,24},{24,20... | collective-permute-start | bytes 1966088 | tf_op jit(solution)/shard_map/ppermute | solution.py:775
  75.7 27.1 %collective-permute-start.9 = (bf16[2,512,256]{2,1,0:T(8,128)(2,1)S(1)}, bf16[2,512,256]{2,1,0:T(8,128)(2,1)}, u32[]{:S(2)}, u32[]{:S(2)}) collective-permute-start(bf16[2,512,256]{2,1,0:T(8,128)(2,1)S(1)} %get-tuple-element.46), channel_id=1, source_target_pairs={{4,6},{6,4},{5,7},{7,5},{8,10},{10,8},{9,11},{11,9},{20,22},{22,20... | collective-permute-start | bytes 1572872 | tf_op jit(solution)/shard_map/ppermute | solution.py:814
  87.0 36.5 %collective-permute-start = (bf16[4,2,4,64,256]{4,3,2,1,0:T(8,128)(2,1)}, bf16[4,2,4,64,256]{4,3,2,1,0:T(8,128)(2,1)S(1)}, u32[]{:S(2)}, u32[]{:S(2)}) collective-permute-start(bf16[4,2,4,64,256]{4,3,2,1,0:T(8,128)(2,1)} %near_rows.1), channel_id=1, source_target_pairs={{4,0},{8,12},{5,1},{9,13},{6,2},{10,14},{7,3},{11,15},{20,16},{24,... | collective-permute-start | bytes 3145736 | tf_op jit(solution)/shard_map/ppermute | solution.py:766
  88.3 63.3 %collective-permute-start.2 = (bf16[2,2,10,64,256]{4,3,2,1,0:T(8,128)(2,1)}, bf16[2,2,10,64,256]{4,3,2,1,0:T(8,128)(2,1)S(1)}, u32[]{:S(2)}, u32[]{:S(2)}) collective-permute-start(bf16[2,2,10,64,256]{4,3,2,1,0:T(8,128)(2,1)} %collective-permute-done.1.refs_1_.far_near_ref), channel_id=1, source_target_pairs={{4,0},{8,12},{5,1},{9,13},{6,2},{10,14},{7,3},{11,15},{20,16},{24,... | collective-permute-start | bytes 3932168 | tf_op jit(solution)/shard_map/ppermute | solution.py:777
  99.9 79.8 %collective-permute-start.5 = (bf16[2,2,10,64,256]{4,3,2,1,0:T(8,128)(2,1)}, bf16[2,2,10,64,256]{4,3,2,1,0:T(8,128)(2,1)S(1)}, u32[]{:S(2)}, u32[]{:S(2)}) collective-permute-start(bf16[2,2,10,64,256]{4,3,2,1,0:T(8,128)(2,1)} %collective-permute-done.4.refs_2_.far_far_ref), channel_id=1, source_target_pairs={{4,0},{8,12},{5,1},{9,13},{6,2},{10,14},{7,3},{11,15},{20,16},{24,... | collective-permute-start | bytes 3932168 | tf_op jit(solution)/shard_map/ppermute | solution.py:778
  102.2 29.5 %collective-permute-start.15 = (bf16[1,2,10,64,256]{4,3,2,1,0:T(8,128)(2,1)S(1)}, bf16[1,2,10,64,256]{4,3,2,1,0:T(8,128)(2,1)S(1)}, u32[]{:S(2)}, u32[]{:S(2)}) collective-permute-start(bf16[1,2,10,64,256]{4,3,2,1,0:T(8,128)(2,1)S(1)} %collective-permute-done.13.partner_ref.refs_3_), channel_id=1, source_target_pairs={{4,8},{8,4},{5,9},{9,5},{6,10},{10,6},{7,11},{11,7},{20,24},{24,20... | collective-permute-start | bytes 1966088 | tf_op jit(solution)/shard_map/ppermute | solution.py:776
  102.9 30.1 %collective-permute-start.18 = (bf16[1,2,10,64,256]{4,3,2,1,0:T(8,128)(2,1)S(1)}, bf16[1,2,10,64,256]{4,3,2,1,0:T(8,128)(2,1)S(1)}, u32[]{:S(2)}, u32[]{:S(2)}) collective-permute-start(bf16[1,2,10,64,256]{4,3,2,1,0:T(8,128)(2,1)S(1)} %copy-done.2), channel_id=1, source_target_pairs={{4,8},{8,4},{5,9},{9,5},{6,10},{10,6},{7,11},{11,7},{20,24},{24,20... | collective-permute-start | bytes 1966088 | tf_op jit(solution)/shard_map/ppermute | solution.py:776
  123.6 77.0 %collective-permute-start.12 = (bf16[2,512,768]{2,1,0:T(8,128)(2,1)}, bf16[2,512,768]{2,1,0:T(8,128)(2,1)S(1)}, u32[]{:S(2)}, u32[]{:S(2)}) collective-permute-start(bf16[2,512,768]{2,1,0:T(8,128)(2,1)} %shard_map.74), channel_id=1, source_target_pairs={{0,4},{12,8},{1,5},{13,9},{2,6},{14,10},{3,7},{15,11},{16,20},{28,... | collective-permute-start | bytes 4718600 | tf_op jit(solution)/shard_map/ppermute | solution.py:770
  131.7 71.6 %collective-permute-start.24 = (bf16[1,2,10,64,256]{4,3,2,1,0:T(8,128)(2,1)}, bf16[1,2,10,64,256]{4,3,2,1,0:T(8,128)(2,1)S(1)}, u32[]{:S(2)}, u32[]{:S(2)}) collective-permute-start(bf16[1,2,10,64,256]{4,3,2,1,0:T(8,128)(2,1)} %collective-permute-done.14.far_near_ref.refs_4_), channel_id=1, source_target_pairs={{4,0},{8,12},{5,1},{9,13},{6,2},{10,14},{7,3},{11,15},{20,16},{24,... | collective-permute-start | bytes 1966088 | tf_op jit(solution)/shard_map/ppermute | solution.py:777
  133.0 98.4 %collective-permute-start.22 = (bf16[1,2,10,64,256]{4,3,2,1,0:T(8,128)(2,1)}, bf16[1,2,10,64,256]{4,3,2,1,0:T(8,128)(2,1)S(1)}, u32[]{:S(2)}, u32[]{:S(2)}) collective-permute-start(bf16[1,2,10,64,256]{4,3,2,1,0:T(8,128)(2,1)} %collective-permute-done.17.far_near_ref.refs_7_), channel_id=1, source_target_pairs={{4,0},{8,12},{5,1},{9,13},{6,2},{10,14},{7,3},{11,15},{20,16},{24,... | collective-permute-start | bytes 1966088 | tf_op jit(solution)/shard_map/ppermute | solution.py:777
  151.7 70.3 %collective-permute-start.25 = (bf16[1,2,10,64,256]{4,3,2,1,0:T(8,128)(2,1)S(1)}, bf16[1,2,10,64,256]{4,3,2,1,0:T(8,128)(2,1)}, u32[]{:S(2)}, u32[]{:S(2)}) collective-permute-start(bf16[1,2,10,64,256]{4,3,2,1,0:T(8,128)(2,1)S(1)} %collective-permute-done.15.far_far_ref.refs_5_), channel_id=1, source_target_pairs={{4,0},{8,12},{5,1},{9,13},{6,2},{10,14},{7,3},{11,15},{20,16},{24,... | collective-permute-start | bytes 1966088 | tf_op jit(solution)/shard_map/ppermute | solution.py:778
  179.7 52.9 %collective-permute-start.23 = (bf16[1,2,10,64,256]{4,3,2,1,0:T(8,128)(2,1)S(1)}, bf16[1,2,10,64,256]{4,3,2,1,0:T(8,128)(2,1)}, u32[]{:S(2)}, u32[]{:S(2)}) collective-permute-start(bf16[1,2,10,64,256]{4,3,2,1,0:T(8,128)(2,1)S(1)} %collective-permute-done.18.far_far_ref.refs_8_), channel_id=1, source_target_pairs={{4,0},{8,12},{5,1},{9,13},{6,2},{10,14},{7,3},{11,15},{20,16},{24,... | collective-permute-start | bytes 1966088 | tf_op jit(solution)/shard_map/ppermute | solution.py:778
  200.6 46.5 %collective-permute-start.10 = (f32[512,256]{1,0:T(8,128)}, f32[512,256]{1,0:T(8,128)}, u32[]{:S(2)}, u32[]{:S(2)}) collective-permute-start(f32[512,256]{1,0:T(8,128)} %select_bitcast_fusion.1), channel_id=1, source_target_pairs={{4,5},{5,4},{6,7},{7,6},{8,9},{9,8},{10,11},{11,10},{20,21},{21,20... | collective-permute-start | bytes 1572872 | tf_op jit(solution)/shard_map/ppermute | solution.py:819
  249.2 31.4 %collective-permute-start.26 = (bf16[1024,256]{1,0:T(8,128)(2,1)S(1)}, bf16[1024,256]{1,0:T(8,128)(2,1)S(1)}, u32[]{:S(2)}, u32[]{:S(2)}) collective-permute-start(bf16[1024,256]{1,0:T(8,128)(2,1)S(1)} %get-tuple-element.62), channel_id=1, source_target_pairs={{0,2},{2,0},{1,3},{3,1},{4,6},{6,4},{5,7},{7,5},{8,10},{10,8},{9,1... | collective-permute-start | bytes 1572872 | tf_op jit(solution)/shard_map/ppermute | solution.py:828
  252.4 28.0 %collective-permute-start.29 = (f32[4,64,256]{2,1,0:T(8,128)S(1)}, f32[4,64,256]{2,1,0:T(8,128)S(1)}, u32[]{:S(2)}, u32[]{:S(2)}) collective-permute-start(f32[4,64,256]{2,1,0:T(8,128)S(1)} %constant_dynamic-slice_fusion), channel_id=1, source_target_pairs={{0,2},{2,0},{1,3},{3,1},{4,6},{6,4},{5,7},{7,5},{8,10},{10,8},{9,1... | collective-permute-start | bytes 786440 | tf_op jit(solution)/shard_map/ppermute | solution.py:836
  252.7 37.9 %collective-permute-start.20 = (f32[512,256]{1,0:T(8,128)S(1)}, f32[512,256]{1,0:T(8,128)S(1)}, u32[]{:S(2)}, u32[]{:S(2)}) collective-permute-start(f32[512,256]{1,0:T(8,128)S(1)} %select_bitcast_fusion), channel_id=1, source_target_pairs={{4,5},{5,4},{6,7},{7,6},{8,9},{9,8},{10,11},{11,10},{20,21},{21,20... | collective-permute-start | bytes 1572872 | tf_op jit(solution)/shard_map/ppermute | solution.py:819
  275.4 27.6 %collective-permute-start.8 = (f32[1024,256]{1,0:T(8,128)S(1)}, f32[1024,256]{1,0:T(8,128)}, u32[]{:S(2)}, u32[]{:S(2)}) collective-permute-start(f32[1024,256]{1,0:T(8,128)S(1)} %convert_add_fusion.3), channel_id=1, source_target_pairs={{1,0},{2,3},{5,4},{6,7},{9,8},{10,11},{13,12},{14,15},{17,16},{18,... | collective-permute-start | bytes 3145736 | tf_op jit(solution)/shard_map/ppermute | solution.py:823
  (33 other events, 647.8 us)
where the time goes:
time: 307 us; the launch traced here: 306 us
  waiting for transfers between devices  169 us (55%)
  Pallas kernels  61.2 us (20%)
  starting transfers between devices  57.1 us (19%)
  other arithmetic  11.4 us (4%)
  local copies, waits for them, and re-layouts  6.06 us (2%)
    ppermute x3, waiting for transfers between devices, shards_line(): end_far = lax.ppermute(mid_far, 'grid', OUTWARD_Z)  46.7 us
    pallas_call x8, Pallas kernels, supernode_terms(): pl.pallas_call(functools.partial(supernode_kernel, k, item, role, fresh,...  42.3 us
    ppermute x3, waiting for transfers between devices, shards_line(): swap = lax.ppermute(own, 'grid', INWARD_Z)  28.2 us
    ppermute x2, waiting for transfers between devices, shards_line(): lent.append(lax.ppermute(packed, 'grid', INWARD_Z))  22 us
    ppermute x1, waiting for transfers between devices, shards_line(): lax.ppermute(sent_outer, 'pole', ACROSS_X).astype(jnp.float32)  21.9 us
    ppermute x3, waiting for transfers between devices, shards_line(): end_near = lax.ppermute(mid_near, 'grid', OUTWARD_Z)  17.3 us
    ppermute x1, waiting for transfers between devices, shards_line(): near = lax.ppermute(near_rows, 'grid', OUTWARD_Z)  16.6 us
    pallas_call x2, Pallas kernels, packed_columns(): pl.pallas_call(functools.partial(pack_columns_kernel, depth, width), out_...  13.5 us
  transfers between devices with their start and end apart: 35, of which 15 were waited for; matrix products, arithmetic and copies ran while one was open for 4% of the time, Pallas kernels for 20%

commit v1 on v0

--- a/solution.py
+++ b/solution.py
@@ -285,6 +285,15 @@
                         )
                     )
 
+    def store(part, panel):
+        @pl.when(keeps)
+        def _():
+            out32[part] = panel
+
+        @pl.when(jnp.logical_not(keeps))
+        def _():
+            out16[part] = panel.astype(out16.dtype)
+
     def out_copy(part, action):
         panel_rows = pl.ds(pl.multiple_of(part * width, width), width)
 
@@ -367,8 +376,7 @@
 
             @pl.when(found < 0)
             def _():
-                out32[part] = jnp.zeros((width, width), out32.dtype)
-                out16[part] = jnp.zeros((width, width), out16.dtype)
+                store(part, jnp.zeros((width, width), jnp.float32))
 
             @pl.when(found >= 0)
             def _():
@@ -382,9 +390,7 @@
                 by_imag = plain_product(rows[part, 1], stacked)
                 real = -(by_real[:, :width] - by_imag[:, width:])
                 imag = -(by_real[:, width:] + by_imag[:, :width])
-                panel = weight_real * imag + weight_imag * real
-                out32[part] = panel
-                out16[part] = panel.astype(out16.dtype)
+                store(part, weight_real * imag + weight_imag * real)
                 add_diagonal(
                     found,
                     jnp.concatenate([real.astype(jnp.bfloat16), imag.astype(jnp.bfloat16)], axis=1),
@@ -454,7 +460,7 @@
             pltpu.SemaphoreType.DMA,
             pltpu.SemaphoreType.DMA,
         ],
-        compiler_params=pltpu.CompilerParams(vmem_limit_bytes=52 * 1024 * 1024),
+        compiler_params=pltpu.CompilerParams(vmem_limit_bytes=48 * 1024 * 1024),
         cost_estimate=pl.CostEstimate(
             flops=8 * height * width * width * listed_count,
             bytes_accessed=6 * height * width * listed_count,
@@ -500,7 +506,7 @@
     supers, width, _ = total.shape
     depth = tiles_ref.shape[4]
     slices = columns.shape[1] // width
-    others = factors.shape[1] // depth
+    others = factors.shape[2] // depth
     place = place_ref[0]
     edge = place_ref[1]
     first_half = place_ref[2]
@@ -530,16 +536,15 @@
 
                 @pl.when(found >= 0)
                 def _():
-                    for part in range(2):
-                        pltpu.make_async_copy(
-                            tiles_ref.at[0, k, part, found],
-                            factors.at[k, span, pl.ds(part * width, width)],
-                            factor_sems.at[k, other],
-                        ).start()
+                    pltpu.make_async_copy(
+                        tiles_ref.at[0, k, :, found],
+                        factors.at[k, :, span, :],
+                        factor_sems.at[k, other],
+                    ).start()
 
                 @pl.when(found < 0)
                 def _():
-                    factors[k, span, :] = jnp.zeros((depth, 2 * width), factors.dtype)
+                    factors[k, :, span, :] = jnp.zeros((2, depth, width), factors.dtype)
 
         for chunk, group in enumerate(CHUNKS[:known]):
             swap_ref, near_ref, far_ref = part_refs[chunk]
@@ -599,7 +604,7 @@
                 @pl.when(table_ref[k, other_first + other] >= 0)
                 def _():
                     pltpu.make_async_copy(
-                        factors.at[k, span, :], factors.at[k, span, :], factor_sems.at[k, other]
+                        factors.at[k, :, span, :], factors.at[k, :, span, :], factor_sems.at[k, other]
                     ).wait()
 
             slot = lax.rem(k, 2)
@@ -625,8 +630,9 @@
 
                 @pl.when(found >= 0)
                 def _():
-                    by_real = plain_product(columns[0, panel_rows, :], factors[k])
-                    by_imag = plain_product(columns[1, panel_rows, :], factors[k])
+                    stacked = jnp.concatenate([factors[k, 0], factors[k, 1]], axis=1)
+                    by_real = plain_product(columns[0, panel_rows, :], stacked)
+                    by_imag = plain_product(columns[1, panel_rows, :], stacked)
                     real = -(by_real[:, :width] - by_imag[:, width:])
                     imag = -(by_real[:, width:] + by_imag[:, :width])
                     store(weight_real * imag + weight_imag * real)
@@ -646,7 +652,8 @@
 
                     if pending:
                         is_pending = functools.reduce(jnp.logical_or, [k == p for p in pending])
-                        pl.when(jnp.logical_not(is_pending))(with_diagonal)
+                        if ready:
+                            pl.when(jnp.logical_not(is_pending))(with_diagonal)
                         place_in = sum(
                             jnp.where(k == p, index, 0) for index, p in enumerate(pending)
                         )
@@ -697,7 +704,7 @@
         input_output_aliases={5 + 3 * known: 2} if outputs else {},
         scratch_shapes=[
             pltpu.VMEM(columns.shape, columns.dtype),
-            pltpu.VMEM((supers, others * depth, 2 * width), tiles.dtype),
+            pltpu.VMEM((supers, 2, others * depth, width), tiles.dtype),
             pltpu.VMEM((supers, slices, 2, 4 * depth, width), tiles.dtype),
             pltpu.VMEM((2, slices, width, width), jnp.bfloat16),
             pltpu.VMEM((2, slices, width, width), jnp.float32),
@@ -710,7 +717,7 @@
             pltpu.SemaphoreType.DMA,
             pltpu.SemaphoreType.DMA,
         ],
-        compiler_params=pltpu.CompilerParams(vmem_limit_bytes=52 * 1024 * 1024),
+        compiler_params=pltpu.CompilerParams(vmem_limit_bytes=48 * 1024 * 1024),
         cost_estimate=pl.CostEstimate(
             flops=8 * height * supers * width * others * depth,
             bytes_accessed=8 * supers * others * depth * width,
@@ -754,7 +761,6 @@
     def joined(mine, other, which):
         return jnp.where(which == 0, jnp.concatenate([mine, other]), jnp.concatenate([other, mine]))
 
-    owns = [jnp.stack([factor_tiles[0, k] for k in group]) for group in CHUNKS]
     near_rows = pl.pallas_call(
         near_rows_kernel,
         out_shape=jax.ShapeDtypeStruct((supers, 2, slices, depth, width), factor_tiles.dtype),
@@ -763,7 +769,12 @@
         scratch_shapes=[pltpu.SemaphoreType.DMA((supers, slices))],
         name="near_rows",
     )(table, places, factor_tiles)
+    near_rows, later = lax.optimization_barrier((near_rows, factor_tiles))
     near = lax.ppermute(near_rows, "grid", OUTWARD_Z)
+    owns = [
+        jnp.stack([(later if c else factor_tiles)[0, k] for k in group])
+        for c, group in enumerate(CHUNKS)
+    ]
     lent = []
     for half in range(2):
         packed = packed_columns(places, inverse_pool, depth, width, half, 2)
@@ -787,7 +798,7 @@
         swap, mid_near, mid_far, end_near, end_far = parts[c]
         wanted = (near, end_near, end_far) if role else (swap, mid_near, mid_far)
         return supernode_terms(
-            k, CHUNKS[c].index(k), role, k - 1 if columns else None, *common, wanted,
+            k, CHUNKS[c].index(k), role, k if columns else None, *common, wanted,
             diag_inverse, columns, outputs,
         )
 
@@ -798,9 +809,9 @@
         )
 
     lent_sent, lent_kept = [None] * 2, [None] * 2
-    lent_sent[0], lent_kept[0], diag, columns = lent_node(0, 1, ())
-    outer = node(0, 0, (), (diag,))
-    outer = node(3, 0, (), outer)
+    lent_sent[0], lent_kept[0], diag, columns = lent_node(0, 0, ())
+    outer = node(0, 0, (columns,), (diag,))
+    outer = node(3, 0, (columns,), outer)
     outer = node(0, 1, (), outer)
     sent_outer, kept_outer, diag = node(3, 1, (), outer)
     inner = node(1, 0, (columns,), (diag,))
@@ -809,25 +820,27 @@
     sent_inner, kept_inner, diag = node(1, 1, (), (inner[0], inner[1], diag))
     sent_inner, kept_inner, diag = node(2, 1, (), (sent_inner, kept_inner, diag))
 
+    def plus(kept, other):
+        return kept + other.astype(jnp.float32)
+
     returned = []
     for half in range(2):
-        both = lent_kept[half] + lax.ppermute(
-            lent_sent[half], both_axes, planes((1, 2), ACROSS_X)
-        ).astype(jnp.float32)
+        other = lax.ppermute(lent_sent[half], both_axes, planes((1, 2), ACROSS_X))
+        both = plus(lent_kept[half], other)
         mine = jnp.where(core == 0, both[0], both[1])
         yours = jnp.where(core == 0, both[1], both[0])
         mine = mine + lax.ppermute(yours, both_axes, planes((1, 2), PAIRS_Z))
         returned.append(lax.ppermute(mine.astype(jnp.bfloat16), "grid", OUTWARD_Z))
 
-    chip_sum = kept_outer + lax.ppermute(sent_outer, "pole", ACROSS_X).astype(jnp.float32)
-    base = chip_sum + lax.ppermute(chip_sum, "pole", [(1, 0), (2, 3)])
+    chip_sum = plus(kept_outer, lax.ppermute(sent_outer, "pole", ACROSS_X))
+    outer_sum = chip_sum + lax.ppermute(chip_sum, "pole", [(1, 0), (2, 3)])
     in_outer = jnp.logical_or(pole == 0, pole == 3)
+    chip_sum = plus(kept_inner, lax.ppermute(sent_inner, "pole", ACROSS_X))
+    other = lax.ppermute(chip_sum, "pole", [(0, 1), (3, 2)])
     back = jnp.concatenate(returned).astype(jnp.float32)
-    base = jnp.where(in_outer, base, 0.0) + jnp.where(edge, back, 0.0)
-    base = lax.optimization_barrier(base)
-    chip_sum = kept_inner + lax.ppermute(sent_inner, "pole", ACROSS_X).astype(jnp.float32)
-    last = chip_sum + lax.ppermute(chip_sum, "pole", [(0, 1), (3, 2)])
-    panel_share = base + jnp.where(in_outer, 0.0, last)
+    base = jnp.where(edge, back, 0.0) + jnp.where(in_outer, outer_sum, 0.0)
+    base, chip_sum = lax.optimization_barrier((base, chip_sum))
+    panel_share = base + jnp.where(in_outer, 0.0, chip_sum + other)
 
     def to_quarters(value, places_z):
         sent, kept = halves(value, core, 1)

time: 307 us -> 314 us (1.023)
  local copies, waits for them, and re-layouts: 6.06 us -> 10.8 us
    ppermute x1, waiting for transfers between devices: 16.6 us -> 70.6 us  [shards_line(): near = lax.ppermute(near_rows, 'grid', OUTWARD_Z)]
    ppermute x3, waiting for transfers between devices: 46.7 us -> 13.8 us  [shards_line(): end_far = lax.ppermute(mid_far, 'grid', OUTWARD_Z)]
    ppermute x3, waiting for transfers between devices: 17.3 us -> 0.01 us  [shards_line(): end_near = lax.ppermute(mid_near, 'grid', OUTWARD_Z)]
    ppermute x3, starting transfers between devices: 13.2 us -> 19.9 us  [shards_line(): swap = lax.ppermute(own, 'grid', INWARD_Z)]
    ppermute x2, starting transfers between devices: 10.6 us -> 3.99 us  [shards_line(): lent.append(lax.ppermute(packed, 'grid', INWARD_Z))]
    unnamed x45 -> x55, local copies, waits for them, and re-layouts: 0.53 us -> 5.29 us
    ppermute x2, waiting for transfers between devices: 22 us -> 25.6 us  [shards_line(): lent.append(lax.ppermute(packed, 'grid', INWARD_Z))]
  transfers between devices with their start and end apart: 35 -> 35, of which waited for: 15 -> 13; matrix products, arithmetic and copies ran while one was open for 4% -> 5% of each run, Pallas kernels for 20% -> 19%
where the time goes in v1:
time: 314 us; the launch traced here: 313 us
  waiting for transfers between devices  171 us (54%)
  Pallas kernels  58.4 us (19%)
  starting transfers between devices  57.3 us (18%)
  other arithmetic  14 us (4%)
  local copies, waits for them, and re-layouts  10.8 us (3%)
    ppermute x1, waiting for transfers between devices, shards_line(): near = lax.ppermute(near_rows, 'grid', OUTWARD_Z)  70.6 us
    pallas_call x8, Pallas kernels, supernode_terms(): pl.pallas_call(functools.partial(supernode_kernel, k, item, role, fresh,...  39.6 us
    ppermute x2, waiting for transfers between devices, shards_line(): lent.append(lax.ppermute(packed, 'grid', INWARD_Z))  25.6 us
    ppermute x3, waiting for transfers between devices, shards_line(): swap = lax.ppermute(own, 'grid', INWARD_Z)  25.5 us
    ppermute x1, waiting for transfers between devices, shards_line(): chip_sum = plus(kept_outer, lax.ppermute(sent_outer, 'pole', ACROSS_X))  21.6 us
    ppermute x3, starting transfers between devices, shards_line(): swap = lax.ppermute(own, 'grid', INWARD_Z)  19.9 us
    ppermute x3, waiting for transfers between devices, shards_line(): end_far = lax.ppermute(mid_far, 'grid', OUTWARD_Z)  13.8 us
    pallas_call x2, Pallas kernels, packed_columns(): pl.pallas_call(functools.partial(pack_columns_kernel, depth, width), out_...  13.4 us
  transfers between devices with their start and end apart: 35, of which 13 were waited for; matrix products, arithmetic and copies ran while one was open for 5% of the time, Pallas kernels for 19%

profile of v1, /device:TPU:0, one launch (start us, length us, event | category | flops | bytes accessed | tf_op | source)
XLA Modules:
  0.0 313.0 jit_solution(8525350540535959154)
XLA Ops:
  3.3 5.0 %collective-permute-start.5 = (bf16[2,2,10,64,256]{4,3,2,1,0:T(8,128)(2,1)}, bf16[2,2,10,64,256]{4,3,2,1,0:T(8,128)(2,1)S(1)}, u32[]{:S(2)}, u32[]{:S(2)}) collective-permute-start(bf16[2,2,10,64,256]{4,3,2,1,0:T(8,128)(2,1)} %pad_maximum_fusion), channel_id=1, source_target_pairs={{0,4},{12,8},{1,5},{13,9},{2,6},{14,10},{3,7},{15,11},{16,20},{28,... | collective-permute-start | bytes 3932168 | tf_op jit(solution)/shard_map/ppermute | solution.py:785
  9.0 6.8 %shard_map.68 = bf16[2,512,768]{2,1,0:T(8,128)(2,1)} custom-call(s32[6]{0:T(128)} %stack.34.place_ref, bf16[1,2,1024,4096]{3,2,1,0:T(8,128)(2,1)} %pool_ref.19), custom_call_target="tpu_custom_call" | custom-call | bytes 12582912 | tf_op jit(solution)/shard_map/pallas_call | solution.py:176
  15.8 2.5 collective-permute-start
  20.0 17.7 %collective-permute-done.5.partner_ref.refs_0_ = bf16[2,2,10,64,256]{4,3,2,1,0:T(8,128)(2,1)S(1)} collective-permute-done((bf16[2,2,10,64,256]{4,3,2,1,0:T(8,128)(2,1)}, bf16[2,2,10,64,256]{4,3,2,1,0:T(8,128)(2,1)S(1)}, u32[]{:S(2)}, u32[]{:S(2)}) %collective-permute-start.5) | collective-permute-done | bytes 1310752 | tf_op jit(solution)/shard_map/ppermute | solution.py:785
  40.2 3.0 near_rows.1
  43.2 2.6 slice_bitcast_fusion
  45.8 6.1 %collective-permute-start.8 = (bf16[1,2,10,64,256]{4,3,2,1,0:T(8,128)(2,1)}, bf16[1,2,10,64,256]{4,3,2,1,0:T(8,128)(2,1)S(1)}, u32[]{:S(2)}, u32[]{:S(2)}) collective-permute-start(bf16[1,2,10,64,256]{4,3,2,1,0:T(8,128)(2,1)} %get-tuple-element.73), channel_id=1, source_target_pairs={{0,4},{12,8},{1,5},{13,9},{2,6},{14,10},{3,7},{15,11},{16,20},{28,... | collective-permute-start | bytes 1966088 | tf_op jit(solution)/shard_map/ppermute | solution.py:785
  51.9 19.5 %collective-permute-done.columns_ref = bf16[2,512,768]{2,1,0:T(8,128)(2,1)} collective-permute-done((bf16[2,512,768]{2,1,0:T(8,128)(2,1)}, bf16[2,512,768]{2,1,0:T(8,128)(2,1)}, u32[]{:S(2)}, u32[]{:S(2)}) %collective-permute-start) | collective-permute-done | bytes 1572896 | tf_op jit(solution)/shard_map/ppermute | solution.py:781
  76.6 7.8 %collective-permute-done.8.partner_ref.refs_3_ = bf16[1,2,10,64,256]{4,3,2,1,0:T(8,128)(2,1)S(1)} collective-permute-done((bf16[1,2,10,64,256]{4,3,2,1,0:T(8,128)(2,1)}, bf16[1,2,10,64,256]{4,3,2,1,0:T(8,128)(2,1)S(1)}, u32[]{:S(2)}, u32[]{:S(2)}) %collective-permute-start.8) | collective-permute-done | bytes 655392 | tf_op jit(solution)/shard_map/ppermute | solution.py:785
  84.3 8.8 %collective-permute-start.11 = (bf16[1,2,10,64,256]{4,3,2,1,0:T(8,128)(2,1)}, bf16[1,2,10,64,256]{4,3,2,1,0:T(8,128)(2,1)}, u32[]{:S(2)}, u32[]{:S(2)}) collective-permute-start(bf16[1,2,10,64,256]{4,3,2,1,0:T(8,128)(2,1)} %get-tuple-element.72), channel_id=1, source_target_pairs={{0,4},{12,8},{1,5},{13,9},{2,6},{14,10},{3,7},{15,11},{16,20},{28,... | collective-permute-start | bytes 1966088 | tf_op jit(solution)/shard_map/ppermute | solution.py:785
  93.8 6.6 %shard_map.70 = bf16[2,512,768]{2,1,0:T(8,128)(2,1)} custom-call(s32[6]{0:T(128)} %stack.34.place_ref, bf16[1,2,1024,4096]{3,2,1,0:T(8,128)(2,1)} %pool_ref.19), custom_call_target="tpu_custom_call" | custom-call | bytes 12582912 | tf_op jit(solution)/shard_map/pallas_call | solution.py:176
  110.3 70.6 %collective-permute-done.14.partner_ref = bf16[4,2,4,64,256]{4,3,2,1,0:T(8,128)(2,1)S(1)} collective-permute-done((bf16[4,2,4,64,256]{4,3,2,1,0:T(8,128)(2,1)S(1)}, bf16[4,2,4,64,256]{4,3,2,1,0:T(8,128)(2,1)S(1)}, u32[]{:S(2)}, u32[]{:S(2)}) %collective-permute-start.14) | collective-permute-done | bytes 1048608 | tf_op jit(solution)/shard_map/ppermute | solution.py:773
  187.7 8.8 %shard_map.73 = (bf16[1024,256]{1,0:T(8,128)(2,1)S(1)}, f32[1024,256]{1,0:T(8,128)S(1)}, f32[4,256,256]{2,1,0:T(8,128)S(1)}) custom-call(s32[4,16]{1,0:T(4,128)S(1)} %copy-done.16, s32[4,10]{1,0:T(4,128)S(1)} %copy-done.17, s32[6]{0:T(128)S(1)} %copy-done.19, f32[1,2]{1,0:T(1,128)S(1)} %copy-done.20, ...), custom_call_target="tpu_custom_call", output_to_operand_aliasing={{2}: (12, {}), {0}: (10, {}), {1}: (11, {})} | custom-call | flops 5368709120 | bytes 15728640 | tf_op jit(solution)/shard_map/pallas_call | solution.py:435
  196.5 7.4 %shard_map.74 = (bf16[1024,256]{1,0:T(8,128)(2,1)S(1)}, f32[1024,256]{1,0:T(8,128)S(1)}, f32[4,256,256]{2,1,0:T(8,128)S(1)}) custom-call(s32[4,16]{1,0:T(4,128)S(1)} %copy-done.16, s32[4,10]{1,0:T(4,128)S(1)} %copy-done.17, s32[6]{0:T(128)S(1)} %copy-done.19, f32[1,2]{1,0:T(1,128)S(1)} %copy-done.20, ...), custom_call_target="tpu_custom_call", output_to_operand_aliasing={{2}: (12, {}), {0}: (10, {}), {1}: (11, {})} | custom-call | flops 5368709120 | bytes 15728640 | tf_op jit(solution)/shard_map/pallas_call | solution.py:435
  206.6 6.1 %collective-permute-done.4.columns_ref = bf16[2,512,768]{2,1,0:T(8,128)(2,1)S(1)} collective-permute-done((bf16[2,512,768]{2,1,0:T(8,128)(2,1)}, bf16[2,512,768]{2,1,0:T(8,128)(2,1)S(1)}, u32[]{:S(2)}, u32[]{:S(2)}) %collective-permute-start.4) | collective-permute-done | bytes 1572896 | tf_op jit(solution)/shard_map/ppermute | solution.py:781
  216.5 13.8 %collective-permute-done.25.far_far_ref = bf16[1,2,10,64,256]{4,3,2,1,0:T(8,128)(2,1)S(1)} collective-permute-done((bf16[1,2,10,64,256]{4,3,2,1,0:T(8,128)(2,1)S(1)}, bf16[1,2,10,64,256]{4,3,2,1,0:T(8,128)(2,1)S(1)}, u32[]{:S(2)}, u32[]{:S(2)}) %collective-permute-start.25) | collective-permute-done | bytes 655392 | tf_op jit(solution)/shard_map/ppermute | solution.py:789
  231.5 8.7 %shard_map.78 = (bf16[1024,256]{1,0:T(8,128)(2,1)S(1)}, f32[1024,256]{1,0:T(8,128)S(1)}, f32[4,256,256]{2,1,0:T(8,128)S(1)}) custom-call(s32[4,16]{1,0:T(4,128)S(1)} %copy-done.16, s32[4,10]{1,0:T(4,128)S(1)} %copy-done.17, s32[6]{0:T(128)S(1)} %copy-done.19, f32[1,2]{1,0:T(1,128)S(1)} %copy-done.20, ...), custom_call_target="tpu_custom_call", output_to_operand_aliasing={{2}: (12, {}), {0}: (10, {}), {1}: (11, {})} | custom-call | flops 5368709120 | bytes 15728640 | tf_op jit(solution)/shard_map/pallas_call | solution.py:435
  240.2 11.2 %shard_map.79 = (bf16[1024,256]{1,0:T(8,128)(2,1)S(1)}, f32[1024,256]{1,0:T(8,128)S(1)}, f32[4,256,256]{2,1,0:T(8,128)S(1)}) custom-call(s32[4,16]{1,0:T(4,128)S(1)} %copy-done.16, s32[4,10]{1,0:T(4,128)S(1)} %copy-done.17, s32[6]{0:T(128)S(1)} %copy-done.19, f32[1,2]{1,0:T(1,128)S(1)} %copy-done.20, ...), custom_call_target="tpu_custom_call", output_to_operand_aliasing={{2}: (12, {}), {0}: (10, {}), {1}: (11, {})} | custom-call | flops 5368709120 | bytes 15728640 | tf_op jit(solution)/shard_map/pallas_call | solution.py:435
  260.9 21.6 %collective-permute-done.20 = bf16[1024,256]{1,0:T(8,128)(2,1)S(1)} collective-permute-done((bf16[1024,256]{1,0:T(8,128)(2,1)S(1)}, bf16[1024,256]{1,0:T(8,128)(2,1)S(1)}, u32[]{:S(2)}, u32[]{:S(2)}) %collective-permute-start.20) | collective-permute-done | bytes 524320 | tf_op jit(solution)/shard_map/ppermute | solution.py:835
  284.8 2.8 collective-permute-done.29
  287.8 3.7 %collective-permute-start.32 = (f32[64,256]{1,0:T(8,128)S(1)}, f32[64,256]{1,0:T(8,128)S(1)}, u32[]{:S(2)}, u32[]{:S(2)}) collective-permute-start(f32[64,256]{1,0:T(8,128)S(1)} %get-tuple-element.77), channel_id=1, source_target_pairs={{0,12},{4,0},{8,4},{12,8},{1,13},{5,1},{9,5},{13,9},{2,14},{6,2},{... | collective-permute-start | bytes 196616 | tf_op jit(solution)/shard_map/ppermute | solution.py:855
  291.6 2.8 collective-permute-done.30
  299.6 2.8 collective-permute-done.33
  304.6 4.2 %collective-permute-done.19 = bf16[512,256]{1,0:T(8,128)(2,1)S(1)} collective-permute-done((bf16[512,256]{1,0:T(8,128)(2,1)S(1)}, bf16[512,256]{1,0:T(8,128)(2,1)S(1)}, u32[]{:S(2)}, u32[]{:S(2)}) %collective-permute-start.19) | collective-permute-done | bytes 262176 | tf_op jit(solution)/shard_map/ppermute | solution.py:833
  (137 shorter events, 61.0 us)
Async XLA Ops:
  3.3 34.4 %collective-permute-start.5 = (bf16[2,2,10,64,256]{4,3,2,1,0:T(8,128)(2,1)}, bf16[2,2,10,64,256]{4,3,2,1,0:T(8,128)(2,1)S(1)}, u32[]{:S(2)}, u32[]{:S(2)}) collective-permute-start(bf16[2,2,10,64,256]{4,3,2,1,0:T(8,128)(2,1)} %pad_maximum_fusion), channel_id=1, source_target_pairs={{0,4},{12,8},{1,5},{13,9},{2,6},{14,10},{3,7},{15,11},{16,20},{28,... | collective-permute-start | bytes 3932168 | tf_op jit(solution)/shard_map/ppermute | solution.py:785
  15.8 55.6 %collective-permute-start = (bf16[2,512,768]{2,1,0:T(8,128)(2,1)}, bf16[2,512,768]{2,1,0:T(8,128)(2,1)}, u32[]{:S(2)}, u32[]{:S(2)}) collective-permute-start(bf16[2,512,768]{2,1,0:T(8,128)(2,1)} %shard_map.68), channel_id=1, source_target_pairs={{0,4},{12,8},{1,5},{13,9},{2,6},{14,10},{3,7},{15,11},{16,20},{28,... | collective-permute-start | bytes 4718600 | tf_op jit(solution)/shard_map/ppermute | solution.py:781
  18.2 74.9 %collective-permute-start.6 = (bf16[2,2,10,64,256]{4,3,2,1,0:T(8,128)(2,1)}, bf16[2,2,10,64,256]{4,3,2,1,0:T(8,128)(2,1)}, u32[]{:S(2)}, u32[]{:S(2)}) collective-permute-start(bf16[2,2,10,64,256]{4,3,2,1,0:T(8,128)(2,1)} %pad_maximum_fusion), channel_id=1, source_target_pairs={{4,8},{8,4},{5,9},{9,5},{6,10},{10,6},{7,11},{11,7},{20,24},{24,20... | collective-permute-start | bytes 3932168 | tf_op jit(solution)/shard_map/ppermute | solution.py:786
  37.7 64.1 %collective-permute-start.7 = (bf16[2,2,10,64,256]{4,3,2,1,0:T(8,128)(2,1)S(1)}, bf16[2,2,10,64,256]{4,3,2,1,0:T(8,128)(2,1)}, u32[]{:S(2)}, u32[]{:S(2)}) collective-permute-start(bf16[2,2,10,64,256]{4,3,2,1,0:T(8,128)(2,1)S(1)} %collective-permute-done.5.partner_ref.refs_0_), channel_id=1, source_target_pairs={{4,8},{8,4},{5,9},{9,5},{6,10},{10,6},{7,11},{11,7},{20,24},{24,20... | collective-permute-start | bytes 3932168 | tf_op jit(solution)/shard_map/ppermute | solution.py:787
  45.8 38.5 %collective-permute-start.8 = (bf16[1,2,10,64,256]{4,3,2,1,0:T(8,128)(2,1)}, bf16[1,2,10,64,256]{4,3,2,1,0:T(8,128)(2,1)S(1)}, u32[]{:S(2)}, u32[]{:S(2)}) collective-permute-start(bf16[1,2,10,64,256]{4,3,2,1,0:T(8,128)(2,1)} %get-tuple-element.73), channel_id=1, source_target_pairs={{0,4},{12,8},{1,5},{13,9},{2,6},{14,10},{3,7},{15,11},{16,20},{28,... | collective-permute-start | bytes 1966088 | tf_op jit(solution)/shard_map/ppermute | solution.py:785
  73.6 26.8 %collective-permute-start.1 = (bf16[2,512,256]{2,1,0:T(8,128)(2,1)}, bf16[2,512,256]{2,1,0:T(8,128)(2,1)}, u32[]{:S(2)}, u32[]{:S(2)}) collective-permute-start(bf16[2,512,256]{2,1,0:T(8,128)(2,1)} %get-tuple-element.38), channel_id=1, source_target_pairs={{4,6},{6,4},{5,7},{7,5},{8,10},{10,8},{9,11},{11,9},{20,22},{22,20... | collective-permute-start | bytes 1572872 | tf_op jit(solution)/shard_map/ppermute | solution.py:828
  75.1 29.7 %collective-permute-start.9 = (bf16[1,2,10,64,256]{4,3,2,1,0:T(8,128)(2,1)}, bf16[1,2,10,64,256]{4,3,2,1,0:T(8,128)(2,1)}, u32[]{:S(2)}, u32[]{:S(2)}) collective-permute-start(bf16[1,2,10,64,256]{4,3,2,1,0:T(8,128)(2,1)} %get-tuple-element.73), channel_id=1, source_target_pairs={{4,8},{8,4},{5,9},{9,5},{6,10},{10,6},{7,11},{11,7},{20,24},{24,20... | collective-permute-start | bytes 1966088 | tf_op jit(solution)/shard_map/ppermute | solution.py:786
  84.3 22.6 %collective-permute-start.11 = (bf16[1,2,10,64,256]{4,3,2,1,0:T(8,128)(2,1)}, bf16[1,2,10,64,256]{4,3,2,1,0:T(8,128)(2,1)}, u32[]{:S(2)}, u32[]{:S(2)}) collective-permute-start(bf16[1,2,10,64,256]{4,3,2,1,0:T(8,128)(2,1)} %get-tuple-element.72), channel_id=1, source_target_pairs={{0,4},{12,8},{1,5},{13,9},{2,6},{14,10},{3,7},{15,11},{16,20},{28,... | collective-permute-start | bytes 1966088 | tf_op jit(solution)/shard_map/ppermute | solution.py:785
  100.4 84.7 %collective-permute-start.15 = (bf16[2,2,10,64,256]{4,3,2,1,0:T(8,128)(2,1)}, bf16[2,2,10,64,256]{4,3,2,1,0:T(8,128)(2,1)S(1)}, u32[]{:S(2)}, u32[]{:S(2)}) collective-permute-start(bf16[2,2,10,64,256]{4,3,2,1,0:T(8,128)(2,1)} %collective-permute-done.6.far_near_ref.refs_1_), channel_id=1, source_target_pairs={{4,0},{8,12},{5,1},{9,13},{6,2},{10,14},{7,3},{11,15},{20,16},{24,... | collective-permute-start | bytes 3932168 | tf_op jit(solution)/shard_map/ppermute | solution.py:788
  101.9 84.5 %collective-permute-start.16 = (bf16[2,2,10,64,256]{4,3,2,1,0:T(8,128)(2,1)}, bf16[2,2,10,64,256]{4,3,2,1,0:T(8,128)(2,1)S(1)}, u32[]{:S(2)}, u32[]{:S(2)}) collective-permute-start(bf16[2,2,10,64,256]{4,3,2,1,0:T(8,128)(2,1)} %collective-permute-done.7.far_far_ref.refs_2_), channel_id=1, source_target_pairs={{4,0},{8,12},{5,1},{9,13},{6,2},{10,14},{7,3},{11,15},{20,16},{24,... | collective-permute-start | bytes 3932168 | tf_op jit(solution)/shard_map/ppermute | solution.py:789
  104.8 76.1 %collective-permute-start.14 = (bf16[4,2,4,64,256]{4,3,2,1,0:T(8,128)(2,1)S(1)}, bf16[4,2,4,64,256]{4,3,2,1,0:T(8,128)(2,1)S(1)}, u32[]{:S(2)}, u32[]{:S(2)}) collective-permute-start(bf16[4,2,4,64,256]{4,3,2,1,0:T(8,128)(2,1)S(1)} %copy-done.25), channel_id=1, source_target_pairs={{4,0},{8,12},{5,1},{9,13},{6,2},{10,14},{7,3},{11,15},{20,16},{24,... | collective-permute-start | bytes 3145736 | tf_op jit(solution)/shard_map/ppermute | solution.py:773
  107.0 75.5 %collective-permute-start.10 = (bf16[1,2,10,64,256]{4,3,2,1,0:T(8,128)(2,1)S(1)}, bf16[1,2,10,64,256]{4,3,2,1,0:T(8,128)(2,1)S(1)}, u32[]{:S(2)}, u32[]{:S(2)}) collective-permute-start(bf16[1,2,10,64,256]{4,3,2,1,0:T(8,128)(2,1)S(1)} %copy-done.12), channel_id=1, source_target_pairs={{4,8},{8,4},{5,9},{9,5},{6,10},{10,6},{7,11},{11,7},{20,24},{24,20... | collective-permute-start | bytes 1966088 | tf_op jit(solution)/shard_map/ppermute | solution.py:787
  107.7 76.1 %collective-permute-start.13 = (bf16[1,2,10,64,256]{4,3,2,1,0:T(8,128)(2,1)}, bf16[1,2,10,64,256]{4,3,2,1,0:T(8,128)(2,1)S(1)}, u32[]{:S(2)}, u32[]{:S(2)}) collective-permute-start(bf16[1,2,10,64,256]{4,3,2,1,0:T(8,128)(2,1)} %collective-permute-done.11.partner_ref.refs_6_), channel_id=1, source_target_pairs={{4,8},{8,4},{5,9},{9,5},{6,10},{10,6},{7,11},{11,7},{20,24},{24,20... | collective-permute-start | bytes 1966088 | tf_op jit(solution)/shard_map/ppermute | solution.py:787
  180.9 31.8 %collective-permute-start.4 = (bf16[2,512,768]{2,1,0:T(8,128)(2,1)}, bf16[2,512,768]{2,1,0:T(8,128)(2,1)S(1)}, u32[]{:S(2)}, u32[]{:S(2)}) collective-permute-start(bf16[2,512,768]{2,1,0:T(8,128)(2,1)} %shard_map.70), channel_id=1, source_target_pairs={{0,4},{12,8},{1,5},{13,9},{2,6},{14,10},{3,7},{15,11},{16,20},{28,... | collective-permute-start | bytes 4718600 | tf_op jit(solution)/shard_map/ppermute | solution.py:781
  182.5 34.0 %collective-permute-start.24 = (bf16[1,2,10,64,256]{4,3,2,1,0:T(8,128)(2,1)}, bf16[1,2,10,64,256]{4,3,2,1,0:T(8,128)(2,1)S(1)}, u32[]{:S(2)}, u32[]{:S(2)}) collective-permute-start(bf16[1,2,10,64,256]{4,3,2,1,0:T(8,128)(2,1)} %collective-permute-done.9.far_near_ref.refs_4_), channel_id=1, source_target_pairs={{4,0},{8,12},{5,1},{9,13},{6,2},{10,14},{7,3},{11,15},{20,16},{24,... | collective-permute-start | bytes 1966088 | tf_op jit(solution)/shard_map/ppermute | solution.py:788
  183.8 56.4 %collective-permute-start.22 = (bf16[1,2,10,64,256]{4,3,2,1,0:T(8,128)(2,1)S(1)}, bf16[1,2,10,64,256]{4,3,2,1,0:T(8,128)(2,1)S(1)}, u32[]{:S(2)}, u32[]{:S(2)}) collective-permute-start(bf16[1,2,10,64,256]{4,3,2,1,0:T(8,128)(2,1)S(1)} %copy-done.10), channel_id=1, source_target_pairs={{4,0},{8,12},{5,1},{9,13},{6,2},{10,14},{7,3},{11,15},{20,16},{24,... | collective-permute-start | bytes 1966088 | tf_op jit(solution)/shard_map/ppermute | solution.py:788
  185.1 45.2 %collective-permute-start.25 = (bf16[1,2,10,64,256]{4,3,2,1,0:T(8,128)(2,1)S(1)}, bf16[1,2,10,64,256]{4,3,2,1,0:T(8,128)(2,1)S(1)}, u32[]{:S(2)}, u32[]{:S(2)}) collective-permute-start(bf16[1,2,10,64,256]{4,3,2,1,0:T(8,128)(2,1)S(1)} %collective-permute-done.10.far_far_ref.refs_5_), channel_id=1, source_target_pairs={{4,0},{8,12},{5,1},{9,13},{6,2},{10,14},{7,3},{11,15},{20,16},{24,... | collective-permute-start | bytes 1966088 | tf_op jit(solution)/shard_map/ppermute | solution.py:789
  186.4 53.8 %collective-permute-start.23 = (bf16[1,2,10,64,256]{4,3,2,1,0:T(8,128)(2,1)S(1)}, bf16[1,2,10,64,256]{4,3,2,1,0:T(8,128)(2,1)S(1)}, u32[]{:S(2)}, u32[]{:S(2)}) collective-permute-start(bf16[1,2,10,64,256]{4,3,2,1,0:T(8,128)(2,1)S(1)} %collective-permute-done.13.far_far_ref.refs_8_), channel_id=1, source_target_pairs={{4,0},{8,12},{5,1},{9,13},{6,2},{10,14},{7,3},{11,15},{20,16},{24,... | collective-permute-start | bytes 1966088 | tf_op jit(solution)/shard_map/ppermute | solution.py:789
  212.7 41.3 %collective-permute-start.2 = (f32[512,256]{1,0:T(8,128)}, f32[512,256]{1,0:T(8,128)}, u32[]{:S(2)}, u32[]{:S(2)}) collective-permute-start(f32[512,256]{1,0:T(8,128)} %select_bitcast_fusion.1), channel_id=1, source_target_pairs={{4,5},{5,4},{6,7},{7,6},{8,9},{9,8},{10,11},{11,10},{20,21},{21,20... | collective-permute-start | bytes 1572872 | tf_op jit(solution)/shard_map/ppermute | solution.py:832
  256.2 31.6 %collective-permute-start.26 = (bf16[1024,256]{1,0:T(8,128)(2,1)}, bf16[1024,256]{1,0:T(8,128)(2,1)S(1)}, u32[]{:S(2)}, u32[]{:S(2)}) collective-permute-start(bf16[1024,256]{1,0:T(8,128)(2,1)} %copy-done.8), channel_id=1, source_target_pairs={{0,2},{2,0},{1,3},{3,1},{4,6},{6,4},{5,7},{7,5},{8,10},{10,8},{9,1... | collective-permute-start | bytes 1572872 | tf_op jit(solution)/shard_map/ppermute | solution.py:838
  256.7 25.7 %collective-permute-start.20 = (bf16[1024,256]{1,0:T(8,128)(2,1)S(1)}, bf16[1024,256]{1,0:T(8,128)(2,1)S(1)}, u32[]{:S(2)}, u32[]{:S(2)}) collective-permute-start(bf16[1024,256]{1,0:T(8,128)(2,1)S(1)} %copy-done.7), channel_id=1, source_target_pairs={{0,2},{2,0},{1,3},{3,1},{4,6},{6,4},{5,7},{7,5},{8,10},{10,8},{9,1... | collective-permute-start | bytes 1572872 | tf_op jit(solution)/shard_map/ppermute | solution.py:835
  259.4 28.2 %collective-permute-start.29 = (f32[4,64,256]{2,1,0:T(8,128)S(1)}, f32[4,64,256]{2,1,0:T(8,128)S(1)}, u32[]{:S(2)}, u32[]{:S(2)}) collective-permute-start(f32[4,64,256]{2,1,0:T(8,128)S(1)} %constant_dynamic-slice_fusion), channel_id=1, source_target_pairs={{0,2},{2,0},{1,3},{3,1},{4,6},{6,4},{5,7},{7,5},{8,10},{10,8},{9,1... | collective-permute-start | bytes 786440 | tf_op jit(solution)/shard_map/ppermute | solution.py:849
  260.2 38.1 %collective-permute-start.18 = (f32[512,256]{1,0:T(8,128)S(1)}, f32[512,256]{1,0:T(8,128)S(1)}, u32[]{:S(2)}, u32[]{:S(2)}) collective-permute-start(f32[512,256]{1,0:T(8,128)S(1)} %select_bitcast_fusion), channel_id=1, source_target_pairs={{4,5},{5,4},{6,7},{7,6},{8,9},{9,8},{10,11},{11,10},{20,21},{21,20... | collective-permute-start | bytes 1572872 | tf_op jit(solution)/shard_map/ppermute | solution.py:832
  283.5 25.3 %collective-permute-start.21 = (f32[1024,256]{1,0:T(8,128)}, f32[1024,256]{1,0:T(8,128)}, u32[]{:S(2)}, u32[]{:S(2)}) collective-permute-start(f32[1024,256]{1,0:T(8,128)} %convert_add_fusion.1), channel_id=1, source_target_pairs={{1,0},{2,3},{5,4},{6,7},{9,8},{10,11},{13,12},{14,15},{17,16},{18,... | collective-permute-start | bytes 3145736 | tf_op jit(solution)/shard_map/ppermute | solution.py:836
  (38 other events, 447.5 us)

commit v2 on v1

--- a/solution.py
+++ b/solution.py
@@ -460,7 +460,7 @@
             pltpu.SemaphoreType.DMA,
             pltpu.SemaphoreType.DMA,
         ],
-        compiler_params=pltpu.CompilerParams(vmem_limit_bytes=48 * 1024 * 1024),
+        compiler_params=pltpu.CompilerParams(vmem_limit_bytes=40 * 1024 * 1024),
         cost_estimate=pl.CostEstimate(
             flops=8 * height * width * width * listed_count,
             bytes_accessed=6 * height * width * listed_count,
@@ -717,7 +717,7 @@
             pltpu.SemaphoreType.DMA,
             pltpu.SemaphoreType.DMA,
         ],
-        compiler_params=pltpu.CompilerParams(vmem_limit_bytes=48 * 1024 * 1024),
+        compiler_params=pltpu.CompilerParams(vmem_limit_bytes=40 * 1024 * 1024),
         cost_estimate=pl.CostEstimate(
             flops=8 * height * supers * width * others * depth,
             bytes_accessed=8 * supers * others * depth * width,
@@ -814,11 +814,12 @@
     outer = node(3, 0, (columns,), outer)
     outer = node(0, 1, (), outer)
     sent_outer, kept_outer, diag = node(3, 1, (), outer)
-    inner = node(1, 0, (columns,), (diag,))
-    inner = node(2, 0, (columns,), inner)
-    lent_sent[1], lent_kept[1], diag, _ = lent_node(1, len(CHUNKS), (inner[2],))
-    sent_inner, kept_inner, diag = node(1, 1, (), (inner[0], inner[1], diag))
-    sent_inner, kept_inner, diag = node(2, 1, (), (sent_inner, kept_inner, diag))
+    *inner, diag = node(1, 0, (columns,), (diag,))
+    lent_sent[1], lent_kept[1], diag, _ = lent_node(1, len(CHUNKS), (diag,))
+    inner = node(2, 0, (columns,), (*inner, diag))
+    inner = node(1, 1, (), inner)
+    *inner, diag = node(2, 1, (), inner)
+    sent_inner, kept_inner = inner
 
     def plus(kept, other):
         return kept + other.astype(jnp.float32)

time: 314 us -> 302 us (0.962)
  waiting for transfers between devices: 171 us -> 159 us
    ppermute x1, waiting for transfers between devices: 70.6 us -> 11.9 us  [shards_line(): near = lax.ppermute(near_rows, 'grid', OUTWARD_Z)]
    ppermute x3, waiting for transfers between devices: 13.8 us -> 45.7 us  [shards_line(): end_far = lax.ppermute(mid_far, 'grid', OUTWARD_Z)]
    ppermute x3, waiting for transfers between devices: 0.01 us -> 22.9 us  [shards_line(): end_near = lax.ppermute(mid_near, 'grid', OUTWARD_Z)]
    ppermute x2, waiting for transfers between devices: 25.6 us -> 19.3 us  [shards_line(): lent.append(lax.ppermute(packed, 'grid', INWARD_Z))]
    unnamed x55 -> x61, local copies, waits for them, and re-layouts: 5.29 us -> 7.53 us
  transfers between devices with their start and end apart: 35 -> 35, of which waited for: 13 -> 14; matrix products, arithmetic and copies ran while one was open for 5% -> 4% of each run, Pallas kernels for 19% -> 19%
where the time goes in v2:
time: 302 us; the launch traced here: 301 us
  waiting for transfers between devices  159 us (53%)
  Pallas kernels  58.5 us (19%)
  starting transfers between devices  58.1 us (19%)
  other arithmetic  12 us (4%)
  local copies, waits for them, and re-layouts  11.4 us (4%)
    ppermute x3, waiting for transfers between devices, shards_line(): end_far = lax.ppermute(mid_far, 'grid', OUTWARD_Z)  45.7 us
    pallas_call x8, Pallas kernels, supernode_terms(): pl.pallas_call(functools.partial(supernode_kernel, k, item, role, fresh,...  39.6 us
    ppermute x3, waiting for transfers between devices, shards_line(): swap = lax.ppermute(own, 'grid', INWARD_Z)  24.7 us
    ppermute x3, waiting for transfers between devices, shards_line(): end_near = lax.ppermute(mid_near, 'grid', OUTWARD_Z)  22.9 us
    ppermute x1, waiting for transfers between devices, shards_line(): chip_sum = plus(kept_outer, lax.ppermute(sent_outer, 'pole', ACROSS_X))  20.9 us
    ppermute x2, waiting for transfers between devices, shards_line(): lent.append(lax.ppermute(packed, 'grid', INWARD_Z))  19.3 us
    ppermute x3, starting transfers between devices, shards_line(): swap = lax.ppermute(own, 'grid', INWARD_Z)  18.8 us
    pallas_call x2, Pallas kernels, packed_columns(): pl.pallas_call(functools.partial(pack_columns_kernel, depth, width), out_...  13.3 us
  transfers between devices with their start and end apart: 35, of which 14 were waited for; matrix products, arithmetic and copies ran while one was open for 4% of the time, Pallas kernels for 19%

profile of v2, /device:TPU:0, one launch (start us, length us, event | category | flops | bytes accessed | tf_op | source)
XLA Modules:
  0.0 300.6 jit_solution(15183039097261112855)
XLA Ops:
  3.3 6.0 %collective-permute-start.5 = (bf16[2,2,10,64,256]{4,3,2,1,0:T(8,128)(2,1)}, bf16[2,2,10,64,256]{4,3,2,1,0:T(8,128)(2,1)}, u32[]{:S(2)}, u32[]{:S(2)}) collective-permute-start(bf16[2,2,10,64,256]{4,3,2,1,0:T(8,128)(2,1)} %pad_maximum_fusion), channel_id=1, source_target_pairs={{0,4},{12,8},{1,5},{13,9},{2,6},{14,10},{3,7},{15,11},{16,20},{28,... | collective-permute-start | bytes 3932168 | tf_op jit(solution)/shard_map/ppermute | solution.py:785
  10.0 6.7 %shard_map.68 = bf16[2,512,768]{2,1,0:T(8,128)(2,1)} custom-call(s32[6]{0:T(128)} %stack.34.place_ref, bf16[1,2,1024,4096]{3,2,1,0:T(8,128)(2,1)} %pool_ref.19), custom_call_target="tpu_custom_call" | custom-call | bytes 12582912 | tf_op jit(solution)/shard_map/pallas_call | solution.py:176
  16.7 2.5 collective-permute-start
  20.9 16.8 %collective-permute-done.5.partner_ref.refs_0_ = bf16[2,2,10,64,256]{4,3,2,1,0:T(8,128)(2,1)} collective-permute-done((bf16[2,2,10,64,256]{4,3,2,1,0:T(8,128)(2,1)}, bf16[2,2,10,64,256]{4,3,2,1,0:T(8,128)(2,1)}, u32[]{:S(2)}, u32[]{:S(2)}) %collective-permute-start.5) | collective-permute-done | bytes 1310752 | tf_op jit(solution)/shard_map/ppermute | solution.py:785
  40.3 3.1 %near_rows.1 = bf16[4,2,4,64,256]{4,3,2,1,0:T(8,128)(2,1)} custom-call(s32[4,16]{1,0:T(4,128)} %select_reduce_fusion.table_ref, s32[6]{0:T(128)} %stack.34.place_ref, bf16[1,4,2,10,64,256]{5,4,3,2,1,0:T(8,128)(2,1)} %tiles_ref.21), custom_call_target="tpu_custom_call" | custom-call | tf_op jit(solution)/shard_map/near_rows/pallas_call | solution.py:764
  44.4 6.1 %collective-permute-start.8 = (bf16[1,2,10,64,256]{4,3,2,1,0:T(8,128)(2,1)S(1)}, bf16[1,2,10,64,256]{4,3,2,1,0:T(8,128)(2,1)S(1)}, u32[]{:S(2)}, u32[]{:S(2)}) collective-permute-start(bf16[1,2,10,64,256]{4,3,2,1,0:T(8,128)(2,1)S(1)} %get-tuple-element.73), channel_id=1, source_target_pairs={{0,4},{12,8},{1,5},{13,9},{2,6},{14,10},{3,7},{15,11},{16,20},{28,... | collective-permute-start | bytes 1966088 | tf_op jit(solution)/shard_map/ppermute | solution.py:785
  52.1 19.3 %collective-permute-done.columns_ref = bf16[2,512,768]{2,1,0:T(8,128)(2,1)} collective-permute-done((bf16[2,512,768]{2,1,0:T(8,128)(2,1)}, bf16[2,512,768]{2,1,0:T(8,128)(2,1)}, u32[]{:S(2)}, u32[]{:S(2)}) %collective-permute-start) | collective-permute-done | bytes 1572896 | tf_op jit(solution)/shard_map/ppermute | solution.py:781
  76.4 7.8 %collective-permute-done.8.partner_ref.refs_3_ = bf16[1,2,10,64,256]{4,3,2,1,0:T(8,128)(2,1)S(1)} collective-permute-done((bf16[1,2,10,64,256]{4,3,2,1,0:T(8,128)(2,1)S(1)}, bf16[1,2,10,64,256]{4,3,2,1,0:T(8,128)(2,1)S(1)}, u32[]{:S(2)}, u32[]{:S(2)}) %collective-permute-start.8) | collective-permute-done | bytes 655392 | tf_op jit(solution)/shard_map/ppermute | solution.py:785
  84.2 6.7 %collective-permute-start.11 = (bf16[1,2,10,64,256]{4,3,2,1,0:T(8,128)(2,1)}, bf16[1,2,10,64,256]{4,3,2,1,0:T(8,128)(2,1)}, u32[]{:S(2)}, u32[]{:S(2)}) collective-permute-start(bf16[1,2,10,64,256]{4,3,2,1,0:T(8,128)(2,1)} %get-tuple-element.72), channel_id=1, source_target_pairs={{0,4},{12,8},{1,5},{13,9},{2,6},{14,10},{3,7},{15,11},{16,20},{28,... | collective-permute-start | bytes 1966088 | tf_op jit(solution)/shard_map/ppermute | solution.py:785
  93.0 6.6 %shard_map.70 = bf16[2,512,768]{2,1,0:T(8,128)(2,1)} custom-call(s32[6]{0:T(128)} %stack.34.place_ref, bf16[1,2,1024,4096]{3,2,1,0:T(8,128)(2,1)} %pool_ref.19), custom_call_target="tpu_custom_call" | custom-call | bytes 12582912 | tf_op jit(solution)/shard_map/pallas_call | solution.py:176
  107.9 11.9 %collective-permute-done.14.partner_ref = bf16[4,2,4,64,256]{4,3,2,1,0:T(8,128)(2,1)} collective-permute-done((bf16[4,2,4,64,256]{4,3,2,1,0:T(8,128)(2,1)}, bf16[4,2,4,64,256]{4,3,2,1,0:T(8,128)(2,1)}, u32[]{:S(2)}, u32[]{:S(2)}) %collective-permute-start.14) | collective-permute-done | bytes 1048608 | tf_op jit(solution)/shard_map/ppermute | solution.py:773
  125.0 22.9 %collective-permute-done.15.far_near_ref = bf16[2,2,10,64,256]{4,3,2,1,0:T(8,128)(2,1)S(1)} collective-permute-done((bf16[2,2,10,64,256]{4,3,2,1,0:T(8,128)(2,1)}, bf16[2,2,10,64,256]{4,3,2,1,0:T(8,128)(2,1)S(1)}, u32[]{:S(2)}, u32[]{:S(2)}) %collective-permute-start.15) | collective-permute-done | bytes 1310752 | tf_op jit(solution)/shard_map/ppermute | solution.py:788
  149.2 26.8 %collective-permute-done.16.far_far_ref = bf16[2,2,10,64,256]{4,3,2,1,0:T(8,128)(2,1)S(1)} collective-permute-done((bf16[2,2,10,64,256]{4,3,2,1,0:T(8,128)(2,1)}, bf16[2,2,10,64,256]{4,3,2,1,0:T(8,128)(2,1)S(1)}, u32[]{:S(2)}, u32[]{:S(2)}) %collective-permute-start.16) | collective-permute-done | bytes 1310752 | tf_op jit(solution)/shard_map/ppermute | solution.py:789
  177.3 8.6 %shard_map.73 = (bf16[1024,256]{1,0:T(8,128)(2,1)S(1)}, f32[1024,256]{1,0:T(8,128)S(1)}, f32[4,256,256]{2,1,0:T(8,128)S(1)}) custom-call(s32[4,16]{1,0:T(4,128)S(1)} %copy-done.22, s32[4,10]{1,0:T(4,128)S(1)} %copy-done.23, s32[6]{0:T(128)S(1)} %copy-done.25, f32[1,2]{1,0:T(1,128)S(1)} %copy-done.26, ...), custom_call_target="tpu_custom_call", output_to_operand_aliasing={{2}: (12, {}), {0}: (10, {}), {1}: (11, {})} | custom-call | flops 5368709120 | bytes 15728640 | tf_op jit(solution)/shard_map/pallas_call | solution.py:435
  185.9 7.2 %shard_map.74 = (bf16[1024,256]{1,0:T(8,128)(2,1)S(1)}, f32[1024,256]{1,0:T(8,128)S(1)}, f32[4,256,256]{2,1,0:T(8,128)S(1)}) custom-call(s32[4,16]{1,0:T(4,128)S(1)} %copy-done.22, s32[4,10]{1,0:T(4,128)S(1)} %copy-done.23, s32[6]{0:T(128)S(1)} %copy-done.25, f32[1,2]{1,0:T(1,128)S(1)} %copy-done.26, ...), custom_call_target="tpu_custom_call", output_to_operand_aliasing={{2}: (12, {}), {0}: (10, {}), {1}: (11, {})} | custom-call | flops 5368709120 | bytes 15728640 | tf_op jit(solution)/shard_map/pallas_call | solution.py:435
  200.8 17.4 %collective-permute-done.25.far_far_ref = bf16[1,2,10,64,256]{4,3,2,1,0:T(8,128)(2,1)} collective-permute-done((bf16[1,2,10,64,256]{4,3,2,1,0:T(8,128)(2,1)}, bf16[1,2,10,64,256]{4,3,2,1,0:T(8,128)(2,1)}, u32[]{:S(2)}, u32[]{:S(2)}) %collective-permute-start.25) | collective-permute-done | bytes 655392 | tf_op jit(solution)/shard_map/ppermute | solution.py:789
  218.2 8.9 %shard_map.78 = (bf16[1024,256]{1,0:T(8,128)(2,1)S(1)}, f32[1024,256]{1,0:T(8,128)S(1)}, f32[4,256,256]{2,1,0:T(8,128)S(1)}) custom-call(s32[4,16]{1,0:T(4,128)S(1)} %copy-done.22, s32[4,10]{1,0:T(4,128)S(1)} %copy-done.23, s32[6]{0:T(128)S(1)} %copy-done.25, f32[1,2]{1,0:T(1,128)S(1)} %copy-done.26, ...), custom_call_target="tpu_custom_call", output_to_operand_aliasing={{2}: (12, {}), {0}: (10, {}), {1}: (11, {})} | custom-call | flops 5368709120 | bytes 15728640 | tf_op jit(solution)/shard_map/pallas_call | solution.py:435
  228.6 11.3 %shard_map.79 = (bf16[1024,256]{1,0:T(8,128)(2,1)S(1)}, f32[1024,256]{1,0:T(8,128)S(1)}, f32[4,256,256]{2,1,0:T(8,128)S(1)}) custom-call(s32[4,16]{1,0:T(4,128)S(1)} %copy-done.22, s32[4,10]{1,0:T(4,128)S(1)} %copy-done.23, s32[6]{0:T(128)S(1)} %copy-done.25, f32[1,2]{1,0:T(1,128)S(1)} %copy-done.26, ...), custom_call_target="tpu_custom_call", output_to_operand_aliasing={{2}: (12, {}), {0}: (10, {}), {1}: (11, {})} | custom-call | flops 5368709120 | bytes 15728640 | tf_op jit(solution)/shard_map/pallas_call | solution.py:435
  250.1 20.9 %collective-permute-done.20 = bf16[1024,256]{1,0:T(8,128)(2,1)S(1)} collective-permute-done((bf16[1024,256]{1,0:T(8,128)(2,1)S(1)}, bf16[1024,256]{1,0:T(8,128)(2,1)S(1)}, u32[]{:S(2)}, u32[]{:S(2)}) %collective-permute-start.20) | collective-permute-done | bytes 524320 | tf_op jit(solution)/shard_map/ppermute | solution.py:836
  272.5 3.5 %collective-permute-done.29 = f32[4,64,256]{2,1,0:T(8,128)S(1)} collective-permute-done((f32[4,64,256]{2,1,0:T(8,128)S(1)}, f32[4,64,256]{2,1,0:T(8,128)S(1)}, u32[]{:S(2)}, u32[]{:S(2)}) %collective-permute-start.29) | collective-permute-done | bytes 262176 | tf_op jit(solution)/shard_map/ppermute | solution.py:850
  277.3 2.8 collective-permute-start.32
  280.3 2.5 collective-permute-done.30
  288.0 3.0 collective-permute-done.33
  293.1 3.7 %collective-permute-done.19 = bf16[512,256]{1,0:T(8,128)(2,1)S(1)} collective-permute-done((bf16[512,256]{1,0:T(8,128)(2,1)S(1)}, bf16[512,256]{1,0:T(8,128)(2,1)S(1)}, u32[]{:S(2)}, u32[]{:S(2)}) %collective-permute-start.19) | collective-permute-done | bytes 262176 | tf_op jit(solution)/shard_map/ppermute | solution.py:834
  (143 shorter events, 66.2 us)
Async XLA Ops:
  3.3 34.4 %collective-permute-start.5 = (bf16[2,2,10,64,256]{4,3,2,1,0:T(8,128)(2,1)}, bf16[2,2,10,64,256]{4,3,2,1,0:T(8,128)(2,1)}, u32[]{:S(2)}, u32[]{:S(2)}) collective-permute-start(bf16[2,2,10,64,256]{4,3,2,1,0:T(8,128)(2,1)} %pad_maximum_fusion), channel_id=1, source_target_pairs={{0,4},{12,8},{1,5},{13,9},{2,6},{14,10},{3,7},{15,11},{16,20},{28,... | collective-permute-start | bytes 3932168 | tf_op jit(solution)/shard_map/ppermute | solution.py:785
  16.7 54.7 %collective-permute-start = (bf16[2,512,768]{2,1,0:T(8,128)(2,1)}, bf16[2,512,768]{2,1,0:T(8,128)(2,1)}, u32[]{:S(2)}, u32[]{:S(2)}) collective-permute-start(bf16[2,512,768]{2,1,0:T(8,128)(2,1)} %shard_map.68), channel_id=1, source_target_pairs={{0,4},{12,8},{1,5},{13,9},{2,6},{14,10},{3,7},{15,11},{16,20},{28,... | collective-permute-start | bytes 4718600 | tf_op jit(solution)/shard_map/ppermute | solution.py:781
  19.2 72.5 %collective-permute-start.6 = (bf16[2,2,10,64,256]{4,3,2,1,0:T(8,128)(2,1)}, bf16[2,2,10,64,256]{4,3,2,1,0:T(8,128)(2,1)}, u32[]{:S(2)}, u32[]{:S(2)}) collective-permute-start(bf16[2,2,10,64,256]{4,3,2,1,0:T(8,128)(2,1)} %pad_maximum_fusion), channel_id=1, source_target_pairs={{4,8},{8,4},{5,9},{9,5},{6,10},{10,6},{7,11},{11,7},{20,24},{24,20... | collective-permute-start | bytes 3932168 | tf_op jit(solution)/shard_map/ppermute | solution.py:786
  37.7 63.1 %collective-permute-start.7 = (bf16[2,2,10,64,256]{4,3,2,1,0:T(8,128)(2,1)}, bf16[2,2,10,64,256]{4,3,2,1,0:T(8,128)(2,1)}, u32[]{:S(2)}, u32[]{:S(2)}) collective-permute-start(bf16[2,2,10,64,256]{4,3,2,1,0:T(8,128)(2,1)} %collective-permute-done.5.partner_ref.refs_0_), channel_id=1, source_target_pairs={{4,8},{8,4},{5,9},{9,5},{6,10},{10,6},{7,11},{11,7},{20,24},{24,20... | collective-permute-start | bytes 3932168 | tf_op jit(solution)/shard_map/ppermute | solution.py:787
  44.4 39.8 %collective-permute-start.8 = (bf16[1,2,10,64,256]{4,3,2,1,0:T(8,128)(2,1)S(1)}, bf16[1,2,10,64,256]{4,3,2,1,0:T(8,128)(2,1)S(1)}, u32[]{:S(2)}, u32[]{:S(2)}) collective-permute-start(bf16[1,2,10,64,256]{4,3,2,1,0:T(8,128)(2,1)S(1)} %get-tuple-element.73), channel_id=1, source_target_pairs={{0,4},{12,8},{1,5},{13,9},{2,6},{14,10},{3,7},{15,11},{16,20},{28,... | collective-permute-start | bytes 1966088 | tf_op jit(solution)/shard_map/ppermute | solution.py:785
  50.5 40.4 %collective-permute-start.9 = (bf16[1,2,10,64,256]{4,3,2,1,0:T(8,128)(2,1)S(1)}, bf16[1,2,10,64,256]{4,3,2,1,0:T(8,128)(2,1)}, u32[]{:S(2)}, u32[]{:S(2)}) collective-permute-start(bf16[1,2,10,64,256]{4,3,2,1,0:T(8,128)(2,1)S(1)} %get-tuple-element.73), channel_id=1, source_target_pairs={{4,8},{8,4},{5,9},{9,5},{6,10},{10,6},{7,11},{11,7},{20,24},{24,20... | collective-permute-start | bytes 1966088 | tf_op jit(solution)/shard_map/ppermute | solution.py:786
  74.9 24.6 %collective-permute-start.1 = (bf16[2,512,256]{2,1,0:T(8,128)(2,1)}, bf16[2,512,256]{2,1,0:T(8,128)(2,1)}, u32[]{:S(2)}, u32[]{:S(2)}) collective-permute-start(bf16[2,512,256]{2,1,0:T(8,128)(2,1)} %get-tuple-element.38), channel_id=1, source_target_pairs={{4,6},{6,4},{5,7},{7,5},{8,10},{10,8},{9,11},{11,9},{20,22},{22,20... | collective-permute-start | bytes 1572872 | tf_op jit(solution)/shard_map/ppermute | solution.py:829
  84.2 20.5 %collective-permute-start.11 = (bf16[1,2,10,64,256]{4,3,2,1,0:T(8,128)(2,1)}, bf16[1,2,10,64,256]{4,3,2,1,0:T(8,128)(2,1)}, u32[]{:S(2)}, u32[]{:S(2)}) collective-permute-start(bf16[1,2,10,64,256]{4,3,2,1,0:T(8,128)(2,1)} %get-tuple-element.72), channel_id=1, source_target_pairs={{0,4},{12,8},{1,5},{13,9},{2,6},{14,10},{3,7},{15,11},{16,20},{28,... | collective-permute-start | bytes 1966088 | tf_op jit(solution)/shard_map/ppermute | solution.py:785
  91.7 28.2 %collective-permute-start.14 = (bf16[4,2,4,64,256]{4,3,2,1,0:T(8,128)(2,1)}, bf16[4,2,4,64,256]{4,3,2,1,0:T(8,128)(2,1)}, u32[]{:S(2)}, u32[]{:S(2)}) collective-permute-start(bf16[4,2,4,64,256]{4,3,2,1,0:T(8,128)(2,1)} %near_rows.1), channel_id=1, source_target_pairs={{4,0},{8,12},{5,1},{9,13},{6,2},{10,14},{7,3},{11,15},{20,16},{24,... | collective-permute-start | bytes 3145736 | tf_op jit(solution)/shard_map/ppermute | solution.py:773
  99.5 48.3 %collective-permute-start.15 = (bf16[2,2,10,64,256]{4,3,2,1,0:T(8,128)(2,1)}, bf16[2,2,10,64,256]{4,3,2,1,0:T(8,128)(2,1)S(1)}, u32[]{:S(2)}, u32[]{:S(2)}) collective-permute-start(bf16[2,2,10,64,256]{4,3,2,1,0:T(8,128)(2,1)} %collective-permute-done.6.far_near_ref.refs_1_), channel_id=1, source_target_pairs={{4,0},{8,12},{5,1},{9,13},{6,2},{10,14},{7,3},{11,15},{20,16},{24,... | collective-permute-start | bytes 3932168 | tf_op jit(solution)/shard_map/ppermute | solution.py:788
  100.8 75.1 %collective-permute-start.16 = (bf16[2,2,10,64,256]{4,3,2,1,0:T(8,128)(2,1)}, bf16[2,2,10,64,256]{4,3,2,1,0:T(8,128)(2,1)S(1)}, u32[]{:S(2)}, u32[]{:S(2)}) collective-permute-start(bf16[2,2,10,64,256]{4,3,2,1,0:T(8,128)(2,1)} %collective-permute-done.7.far_far_ref.refs_2_), channel_id=1, source_target_pairs={{4,0},{8,12},{5,1},{9,13},{6,2},{10,14},{7,3},{11,15},{20,16},{24,... | collective-permute-start | bytes 3932168 | tf_op jit(solution)/shard_map/ppermute | solution.py:789
  104.7 17.6 %collective-permute-start.10 = (bf16[1,2,10,64,256]{4,3,2,1,0:T(8,128)(2,1)S(1)}, bf16[1,2,10,64,256]{4,3,2,1,0:T(8,128)(2,1)}, u32[]{:S(2)}, u32[]{:S(2)}) collective-permute-start(bf16[1,2,10,64,256]{4,3,2,1,0:T(8,128)(2,1)S(1)} %copy-done.18), channel_id=1, source_target_pairs={{4,8},{8,4},{5,9},{9,5},{6,10},{10,6},{7,11},{11,7},{20,24},{24,20... | collective-permute-start | bytes 1966088 | tf_op jit(solution)/shard_map/ppermute | solution.py:787
  106.2 17.4 %collective-permute-start.13 = (bf16[1,2,10,64,256]{4,3,2,1,0:T(8,128)(2,1)}, bf16[1,2,10,64,256]{4,3,2,1,0:T(8,128)(2,1)S(1)}, u32[]{:S(2)}, u32[]{:S(2)}) collective-permute-start(bf16[1,2,10,64,256]{4,3,2,1,0:T(8,128)(2,1)} %collective-permute-done.11.refs_6_.partner_ref), channel_id=1, source_target_pairs={{4,8},{8,4},{5,9},{9,5},{6,10},{10,6},{7,11},{11,7},{20,24},{24,20... | collective-permute-start | bytes 1966088 | tf_op jit(solution)/shard_map/ppermute | solution.py:787
  119.9 74.2 %collective-permute-start.4 = (bf16[2,512,768]{2,1,0:T(8,128)(2,1)S(1)}, bf16[2,512,768]{2,1,0:T(8,128)(2,1)S(1)}, u32[]{:S(2)}, u32[]{:S(2)}) collective-permute-start(bf16[2,512,768]{2,1,0:T(8,128)(2,1)S(1)} %copy-done.29), channel_id=1, source_target_pairs={{0,4},{12,8},{1,5},{13,9},{2,6},{14,10},{3,7},{15,11},{16,20},{28,... | collective-permute-start | bytes 4718600 | tf_op jit(solution)/shard_map/ppermute | solution.py:781
  122.3 78.5 %collective-permute-start.24 = (bf16[1,2,10,64,256]{4,3,2,1,0:T(8,128)(2,1)}, bf16[1,2,10,64,256]{4,3,2,1,0:T(8,128)(2,1)}, u32[]{:S(2)}, u32[]{:S(2)}) collective-permute-start(bf16[1,2,10,64,256]{4,3,2,1,0:T(8,128)(2,1)} %collective-permute-done.9.far_near_ref.refs_4_), channel_id=1, source_target_pairs={{4,0},{8,12},{5,1},{9,13},{6,2},{10,14},{7,3},{11,15},{20,16},{24,... | collective-permute-start | bytes 1966088 | tf_op jit(solution)/shard_map/ppermute | solution.py:788
  123.7 103.5 %collective-permute-start.22 = (bf16[1,2,10,64,256]{4,3,2,1,0:T(8,128)(2,1)S(1)}, bf16[1,2,10,64,256]{4,3,2,1,0:T(8,128)(2,1)S(1)}, u32[]{:S(2)}, u32[]{:S(2)}) collective-permute-start(bf16[1,2,10,64,256]{4,3,2,1,0:T(8,128)(2,1)S(1)} %copy-done.16), channel_id=1, source_target_pairs={{4,0},{8,12},{5,1},{9,13},{6,2},{10,14},{7,3},{11,15},{20,16},{24,... | collective-permute-start | bytes 1966088 | tf_op jit(solution)/shard_map/ppermute | solution.py:788
  147.9 70.3 %collective-permute-start.25 = (bf16[1,2,10,64,256]{4,3,2,1,0:T(8,128)(2,1)}, bf16[1,2,10,64,256]{4,3,2,1,0:T(8,128)(2,1)}, u32[]{:S(2)}, u32[]{:S(2)}) collective-permute-start(bf16[1,2,10,64,256]{4,3,2,1,0:T(8,128)(2,1)} %collective-permute-done.10.far_far_ref.refs_5_), channel_id=1, source_target_pairs={{4,0},{8,12},{5,1},{9,13},{6,2},{10,14},{7,3},{11,15},{20,16},{24,... | collective-permute-start | bytes 1966088 | tf_op jit(solution)/shard_map/ppermute | solution.py:789
  176.0 52.6 %collective-permute-start.23 = (bf16[1,2,10,64,256]{4,3,2,1,0:T(8,128)(2,1)S(1)}, bf16[1,2,10,64,256]{4,3,2,1,0:T(8,128)(2,1)}, u32[]{:S(2)}, u32[]{:S(2)}) collective-permute-start(bf16[1,2,10,64,256]{4,3,2,1,0:T(8,128)(2,1)S(1)} %collective-permute-done.13.refs_8_.far_far_ref), channel_id=1, source_target_pairs={{4,0},{8,12},{5,1},{9,13},{6,2},{10,14},{7,3},{11,15},{20,16},{24,... | collective-permute-start | bytes 1966088 | tf_op jit(solution)/shard_map/ppermute | solution.py:789
  195.3 48.1 %collective-permute-start.2 = (f32[512,256]{1,0:T(8,128)}, f32[512,256]{1,0:T(8,128)}, u32[]{:S(2)}, u32[]{:S(2)}) collective-permute-start(f32[512,256]{1,0:T(8,128)} %select_bitcast_fusion.1), channel_id=1, source_target_pairs={{4,5},{5,4},{6,7},{7,6},{8,9},{9,8},{10,11},{11,10},{20,21},{21,20... | collective-permute-start | bytes 1572872 | tf_op jit(solution)/shard_map/ppermute | solution.py:833
  244.9 32.5 %collective-permute-start.26 = (bf16[1024,256]{1,0:T(8,128)(2,1)S(1)}, bf16[1024,256]{1,0:T(8,128)(2,1)S(1)}, u32[]{:S(2)}, u32[]{:S(2)}) collective-permute-start(bf16[1024,256]{1,0:T(8,128)(2,1)S(1)} %copy-done.14), channel_id=1, source_target_pairs={{0,2},{2,0},{1,3},{3,1},{4,6},{6,4},{5,7},{7,5},{8,10},{10,8},{9,1... | collective-permute-start | bytes 1572872 | tf_op jit(solution)/shard_map/ppermute | solution.py:839
  245.8 25.2 %collective-permute-start.20 = (bf16[1024,256]{1,0:T(8,128)(2,1)S(1)}, bf16[1024,256]{1,0:T(8,128)(2,1)S(1)}, u32[]{:S(2)}, u32[]{:S(2)}) collective-permute-start(bf16[1024,256]{1,0:T(8,128)(2,1)S(1)} %get-tuple-element.57), channel_id=1, source_target_pairs={{0,2},{2,0},{1,3},{3,1},{4,6},{6,4},{5,7},{7,5},{8,10},{10,8},{9,1... | collective-permute-start | bytes 1572872 | tf_op jit(solution)/shard_map/ppermute | solution.py:836
  248.1 27.9 %collective-permute-start.29 = (f32[4,64,256]{2,1,0:T(8,128)S(1)}, f32[4,64,256]{2,1,0:T(8,128)S(1)}, u32[]{:S(2)}, u32[]{:S(2)}) collective-permute-start(f32[4,64,256]{2,1,0:T(8,128)S(1)} %constant_dynamic-slice_fusion), channel_id=1, source_target_pairs={{0,2},{2,0},{1,3},{3,1},{4,6},{6,4},{5,7},{7,5},{8,10},{10,8},{9,1... | collective-permute-start | bytes 786440 | tf_op jit(solution)/shard_map/ppermute | solution.py:850
  249.2 37.3 %collective-permute-start.18 = (f32[512,256]{1,0:T(8,128)S(1)}, f32[512,256]{1,0:T(8,128)S(1)}, u32[]{:S(2)}, u32[]{:S(2)}) collective-permute-start(f32[512,256]{1,0:T(8,128)S(1)} %select_bitcast_fusion), channel_id=1, source_target_pairs={{4,5},{5,4},{6,7},{7,6},{8,9},{9,8},{10,11},{11,10},{20,21},{21,20... | collective-permute-start | bytes 1572872 | tf_op jit(solution)/shard_map/ppermute | solution.py:833
  271.1 25.7 %collective-permute-start.21 = (f32[1024,256]{1,0:T(8,128)S(1)}, f32[1024,256]{1,0:T(8,128)}, u32[]{:S(2)}, u32[]{:S(2)}) collective-permute-start(f32[1024,256]{1,0:T(8,128)S(1)} %convert_add_fusion.1), channel_id=1, source_target_pairs={{1,0},{2,3},{5,4},{6,7},{9,8},{10,11},{13,12},{14,15},{17,16},{18,... | collective-permute-start | bytes 3145736 | tf_op jit(solution)/shard_map/ppermute | solution.py:837
  (41 other events, 321.4 us)
